TPU v7x, 32 devices: a whole 2x2x4 slice. The times are simulated.
32 devices in a mesh: groups: 2 (over y), samp: 4 (over z), feat: 4 (over x, core).
Axes of the slice: x: 2, y: 2, z: 4, core: 2. Of those that a mesh axis runs over, the one named last changes fastest.
Arguments:
- x_blocks: bfloat16 [64, 64, 128, 128], P(('groups', 'samp'), 'feat'), parts along dimension 0, may hold values from -6 to 6
- block_cols: int32 [64, 64], P('groups', 'feat'), parts along dimension 0, may hold values from 0 to 31
- labels: int32 [8192], P('groups'), parts along dimension 0, may hold values from 0 to 63
- group_ids: int32 [8192], P('groups'), parts along dimension 0, may hold values from 0 to 7, as said below
- picks: int32 [3, 32], P(None, 'groups'), parts along dimension 1, may hold values from 0 to 31, as said below
- w_init: float32 [16384, 64], P('feat'), may hold values from -2.253903 to 2.253903
Outputs:
- scores: float32 [8192, 64], P(('groups', 'samp')), parts along dimension 0
- adversary: float32 [16], P('groups'), parts along dimension 0
There are 2 independent parts, one for each index of `groups`. A program takes and returns all parts, laid end to end along the dimension named above; an argument that names none is the same for every part. Nothing has to cross between parts.
Inputs may be any that keep to these rules, and one draw needn't show every extreme that they name: `group_ids`: every row block of 128 samples holds every group at least once. `picks`: the entries of one step are distinct. Row block b is owned by index b // 8 of samp. The k-th aligned block of 4 entries of a step is the list of index k of samp; it names row blocks owned by index k or by the next index along samp (index 0 after the last); between one and 2 entries of each list name the next index's row blocks, exactly 2 in at least one list of every step.
All inputs are finite; a program needn't handle non-finite values.
Results may differ from a plain program's by a relative error of at most 0.00315.
The roundings to bfloat16 on the way count: a program that leaves them out, or rounds other values in their place, can miss the bound.
Values may be sent and summed in bfloat16 or wider, within the bound.
No kernel may reach another device: no remote copies, remote signals or barrier semaphores. Data moves between devices by JAX's collectives and lax.ppermute only.
A program may use at most 64 MiB of HBM per device.

v0:
```python
import jax
import jax.numpy as jnp
from jax import lax
from jax.sharding import PartitionSpec as P

GRP = 8
STEPS = 3


weight_rate = 8.0
adv_rate = 2.0


def per_device(x_blocks, block_cols, labels, group_ids, picks, w_init):
    row_blocks, per_row, block_size, _ = x_blocks.shape
    feat_rows, classes = w_init.shape
    col_blocks = feat_rows // block_size
    total_blocks = block_cols.shape[0]
    feat_count = lax.axis_size("feat")
    my_index = lax.axis_index("samp")
    step_rate = weight_rate * picks.shape[1] / (per_row * feat_count)
    class_range = jnp.arange(classes, dtype=jnp.int32)
    group_range = jnp.arange(GRP, dtype=jnp.int32)
    block_range = jnp.arange(total_blocks, dtype=jnp.int32)
    col_range = jnp.arange(col_blocks, dtype=jnp.int32)
    sample_groups = (group_ids[:, None] == group_range[None, :]).astype(jnp.float32)
    block_groups = jnp.sum(sample_groups.reshape(total_blocks, block_size, GRP), axis=1)
    own_start = my_index * row_blocks
    own_cols = lax.dynamic_slice_in_dim(block_cols, own_start, row_blocks, 0)
    own_labels = lax.dynamic_slice_in_dim(
        labels, own_start * block_size, row_blocks * block_size, 0
    )
    own_groups = lax.dynamic_slice_in_dim(
        group_ids, own_start * block_size, row_blocks * block_size, 0
    )

    def total_logits(x_rows, col_rows, weights_bf):
        tiles = weights_bf.reshape(col_blocks, block_size, classes)[col_rows]
        partial_sum = jnp.einsum(
            "rbij,rbjc->ric", x_rows, tiles, preferred_element_type=jnp.float32
        )
        summed = lax.psum(partial_sum, "feat")
        return summed.reshape(-1, classes)

    def evaluate(row_data, weights_bf, adversary, counts):
        x_rows, col_rows, label_rows, group_rows, mult_rows = row_data
        logits = total_logits(x_rows, col_rows, weights_bf)
        label_hot = (label_rows[:, None] == class_range[None, :]).astype(jnp.float32)
        group_hot = (group_rows[:, None] == group_range[None, :]).astype(jnp.float32)
        log_total = jax.nn.logsumexp(logits, axis=-1)
        cross = log_total - jnp.sum(logits * label_hot, axis=-1)
        probs = jnp.exp(logits - log_total[:, None])
        local_loss = jnp.dot(mult_rows * cross, group_hot, precision=lax.Precision.HIGHEST)
        loss = lax.psum(local_loss, "samp") / counts
        coef = jnp.dot(group_hot, adversary / counts, precision=lax.Precision.HIGHEST) * mult_rows
        dz_rows = (coef[:, None] * (probs - label_hot)).astype(jnp.bfloat16)
        blocks_here = x_rows.shape[0]
        dz_blocks = dz_rows.reshape(blocks_here, block_size, classes)
        grad_tiles = jnp.einsum(
            "rbij,ric->rbjc", x_rows, dz_blocks, preferred_element_type=jnp.float32
        )
        grad_tiles = grad_tiles.reshape(blocks_here * per_row, block_size * classes)
        col_hot = (col_rows.reshape(-1)[:, None] == col_range[None, :]).astype(jnp.float32)
        grad_local = jnp.dot(col_hot.T, grad_tiles, precision=lax.Precision.HIGHEST)
        return (loss, grad_local.reshape(feat_rows, classes))

    def advance(state, grad_local):
        grad_total = lax.psum(grad_local, "samp")
        new_state = state - step_rate * grad_total
        return (new_state, new_state.astype(jnp.bfloat16))

    state = w_init
    weights_bf = w_init.astype(jnp.bfloat16)
    adversary = jnp.full((GRP,), 1.0 / GRP, jnp.float32)
    for step in range(STEPS):
        block_hits = jnp.sum(
            (picks[step][:, None] == block_range[None, :]).astype(jnp.float32), axis=0
        )
        counts = jnp.dot(block_hits, block_groups, precision=lax.Precision.HIGHEST)
        own_hits = lax.dynamic_slice_in_dim(block_hits, own_start, row_blocks, 0)
        row_data = (x_blocks, own_cols, own_labels, own_groups, jnp.repeat(own_hits, block_size))
        loss_first, grad_first = evaluate(row_data, weights_bf, adversary, counts)
        half_state, half_bf = advance(state, grad_first)
        half_adv = jax.nn.softmax(jnp.log(adversary) + adv_rate * loss_first)
        loss_second, grad_second = evaluate(row_data, half_bf, half_adv, counts)
        state, weights_bf = advance(state, grad_second)
        adversary = jax.nn.softmax(jnp.log(adversary) + adv_rate * loss_second)
    return (total_logits(x_blocks, own_cols, weights_bf), adversary)


def solution(mesh):
    in_specs = (
        P(("groups", "samp"), "feat", None, None),
        P("groups", "feat"),
        P("groups"),
        P("groups"),
        P(None, "groups"),
        P("feat", None),
    )
    out_specs = (P(("groups", "samp"), None), P("groups"))
    return jax.shard_map(
        per_device, mesh=mesh, in_specs=in_specs, out_specs=out_specs, check_vma=False
    )
```

profile of v0, /device:TPU:0, one launch (start us, length us, event | category | flops | bytes accessed | tf_op | source)
XLA Modules:
  0.0 841.8 jit_solution(14522523979013200713)
XLA Ops:
  16.2 33.6 %all-reduce.17.cloned.1.call-done = f32[8,128,64]{1,2,0:T(8,128)} async-done(((f32[8,128,64]{1,2,0:T(8,128)}), f32[8,128,64]{1,2,0:T(8,128)}) %all-reduce.17.cloned.1.call-update) | async-done | bytes 262160 | tf_op jit(solution)/shard_map/psum | solution.py:42
  56.8 6.9 copy.85
  63.7 7.9 reshape.440
  80.9 51.9 %all-reduce.19.cloned.1.call-done = f32[4096,64]{0,1:T(8,128)} async-done(((f32[4096,64]{0,1:T(8,128)}), f32[4096,64]{0,1:T(8,128)}) %all-reduce.19.cloned.1.call-update) | async-done | bytes 1048592 | tf_op jit(solution)/shard_map/psum | solution.py:68
  136.3 5.1 convolution_bitcast_fusion.11
  141.5 31.5 %all-reduce.21.cloned.1.call-done = f32[8,128,64]{1,2,0:T(8,128)} async-done(((f32[8,128,64]{1,2,0:T(8,128)}), f32[8,128,64]{1,2,0:T(8,128)}) %all-reduce.21.cloned.1.call-update) | async-done | bytes 262160 | tf_op jit(solution)/shard_map/psum | solution.py:42
  175.8 11.9 %all-reduce.2 = (f32[8]{0:T(128)S(1)}, f32[8]{0:T(128)S(1)}) all-reduce(f32[8]{0:T(128)S(1)} %convolution_bitcast_fusion.21, f32[8]{0:T(128)S(1)} %convolution_bitcast_fusion.20), channel_id=1, replica_groups=mesh['groups'=2,'samp'=4,'feat'=4] {'samp'}, use_global_device_ids=true, to_apply=%region_5.0 | all-reduce | flops 16 | bytes 128 | tf_op jit(solution)/shard_map/psum | solution.py:54
  197.0 6.9 copy.88
  203.9 7.9 reshape.443
  223.0 47.3 %all-reduce.23.cloned.1.call-done = f32[4096,64]{0,1:T(8,128)} async-done(((f32[4096,64]{0,1:T(8,128)}), f32[4096,64]{0,1:T(8,128)}) %all-reduce.23.cloned.1.call-update) | async-done | bytes 1048592 | tf_op jit(solution)/shard_map/psum | solution.py:68
  273.8 5.1 convolution_bitcast_fusion.10
  279.0 31.4 %all-reduce.25.cloned.1.call-done = f32[8,128,64]{1,2,0:T(8,128)} async-done(((f32[8,128,64]{1,2,0:T(8,128)}), f32[8,128,64]{1,2,0:T(8,128)}) %all-reduce.25.cloned.1.call-update) | async-done | bytes 262160 | tf_op jit(solution)/shard_map/psum | solution.py:42
  317.4 6.9 copy.91
  324.3 7.9 reshape.447
  343.7 51.7 %all-reduce.27.cloned.1.call-done = f32[4096,64]{0,1:T(8,128)} async-done(((f32[4096,64]{0,1:T(8,128)}), f32[4096,64]{0,1:T(8,128)}) %all-reduce.27.cloned.1.call-update) | async-done | bytes 1048592 | tf_op jit(solution)/shard_map/psum | solution.py:68
  399.0 5.1 convolution_bitcast_fusion.9
  404.1 31.4 %all-reduce.29.cloned.1.call-done = f32[8,128,64]{1,2,0:T(8,128)} async-done(((f32[8,128,64]{1,2,0:T(8,128)}), f32[8,128,64]{1,2,0:T(8,128)}) %all-reduce.29.cloned.1.call-update) | async-done | bytes 262160 | tf_op jit(solution)/shard_map/psum | solution.py:42
  438.4 11.7 %all-reduce.1 = (f32[8]{0:T(128)S(1)}, f32[8]{0:T(128)S(1)}) all-reduce(f32[8]{0:T(128)S(1)} %convolution_bitcast_fusion.19, f32[8]{0:T(128)S(1)} %convolution_bitcast_fusion.18), channel_id=1, replica_groups=mesh['groups'=2,'samp'=4,'feat'=4] {'samp'}, use_global_device_ids=true, to_apply=%region_23.0 | all-reduce | flops 16 | bytes 128 | tf_op jit(solution)/shard_map/psum | solution.py:54
  455.6 5.0 convolution_bitcast_fusion.2
  460.6 6.9 copy.94
  467.5 7.9 reshape.450
  489.7 46.1 %all-reduce.31.cloned.1.call-done = f32[4096,64]{0,1:T(8,128)} async-done(((f32[4096,64]{0,1:T(8,128)}), f32[4096,64]{0,1:T(8,128)}) %all-reduce.31.cloned.1.call-update) | async-done | bytes 1048592 | tf_op jit(solution)/shard_map/psum | solution.py:68
  544.2 31.1 %all-reduce.33.cloned.1.call-done = f32[8,128,64]{1,2,0:T(8,128)} async-done(((f32[8,128,64]{1,2,0:T(8,128)}), f32[8,128,64]{1,2,0:T(8,128)}) %all-reduce.33.cloned.1.call-update) | async-done | bytes 262160 | tf_op jit(solution)/shard_map/psum | solution.py:42
  582.3 6.9 copy.97
  589.2 7.9 reshape.454
  606.3 51.9 %all-reduce.35.cloned.1.call-done = f32[4096,64]{0,1:T(8,128)} async-done(((f32[4096,64]{0,1:T(8,128)}), f32[4096,64]{0,1:T(8,128)}) %all-reduce.35.cloned.1.call-update) | async-done | bytes 1048592 | tf_op jit(solution)/shard_map/psum | solution.py:68
  665.1 31.5 %all-reduce.37.cloned.1.call-done = f32[8,128,64]{1,2,0:T(8,128)} async-done(((f32[8,128,64]{1,2,0:T(8,128)}), f32[8,128,64]{1,2,0:T(8,128)}) %all-reduce.37.cloned.1.call-update) | async-done | bytes 262160 | tf_op jit(solution)/shard_map/psum | solution.py:42
  699.5 11.7 %all-reduce = (f32[8]{0:T(128)S(1)}, f32[8]{0:T(128)S(1)}) all-reduce(f32[8]{0:T(128)S(1)} %convolution_bitcast_fusion.17, f32[8]{0:T(128)S(1)} %convolution_bitcast_fusion.16), channel_id=1, replica_groups=mesh['groups'=2,'samp'=4,'feat'=4] {'samp'}, use_global_device_ids=true, to_apply=%region_40.0 | all-reduce | flops 16 | bytes 128 | tf_op jit(solution)/shard_map/psum | solution.py:54
  721.6 6.9 copy.100
  728.5 7.9 reshape.457
  746.9 47.9 %all-reduce.39.cloned.1.call-done = f32[4096,64]{0,1:T(8,128)} async-done(((f32[4096,64]{0,1:T(8,128)}), f32[4096,64]{0,1:T(8,128)}) %all-reduce.39.cloned.1.call-update) | async-done | bytes 1048592 | tf_op jit(solution)/shard_map/psum | solution.py:68
  803.5 29.7 %all-reduce.41.cloned.1.call-done = f32[1024,64]{0,1:T(8,128)} async-done(((f32[1024,64]{0,1:T(8,128)}), f32[1024,64]{0,1:T(8,128)}) %all-reduce.41.cloned.1.call-update) | async-done | bytes 262160 | tf_op jit(solution)/shard_map/psum | solution.py:42
  (161 shorter events, 165.8 us)
Async XLA Ops:
  7.2 9.0 %copy-start = (s32[4096]{0:T(1024)S(1)}, s32[4096]{0:T(1024)}, u32[]{:S(2)}) copy-start(s32[4096]{0:T(1024)} %param.8) | copy-start | bytes 49156
  7.2 42.6 %all-reduce.17.cloned.1.call-start = ((), (), s32[]{:S(2)}) async-start(), calls=%async_computation | async-start | bytes 524288 | tf_op jit(solution)/shard_map/psum | solution.py:42
  10.5 4.5 copy-start.7
  10.5 4.7 copy-start.6
  15.0 117.8 %all-reduce.19.cloned.1.call-start = ((), (), s32[]{:S(2)}) async-start(), calls=%async_computation.1 | async-start | bytes 2097152 | tf_op jit(solution)/shard_map/psum | solution.py:68
  75.4 57.4 %copy-start.2 = (f32[4096,64]{0,1:T(8,128)S(1)}, f32[4096,64]{0,1:T(8,128)}, u32[]{:S(2)}) copy-start(f32[4096,64]{0,1:T(8,128)} %param.11) | copy-start | bytes 3145732
  80.8 92.1 %all-reduce.21.cloned.1.call-start = ((), (), s32[]{:S(2)}) async-start(), calls=%async_computation.2 | async-start | bytes 524288 | tf_op jit(solution)/shard_map/psum | solution.py:42
  141.4 128.9 %all-reduce.23.cloned.1.call-start = ((), (), s32[]{:S(2)}) async-start(), calls=%async_computation.3 | async-start | bytes 2097152 | tf_op jit(solution)/shard_map/psum | solution.py:68
  221.0 89.4 %all-reduce.25.cloned.1.call-start = ((), (), s32[]{:S(2)}) async-start(), calls=%async_computation.4 | async-start | bytes 524288 | tf_op jit(solution)/shard_map/psum | solution.py:42
  278.9 116.5 %all-reduce.27.cloned.1.call-start = ((), (), s32[]{:S(2)}) async-start(), calls=%async_computation.5 | async-start | bytes 2097152 | tf_op jit(solution)/shard_map/psum | solution.py:68
  337.0 58.4 %copy-start.3 = (f32[4096,64]{0,1:T(8,128)S(1)}, f32[4096,64]{0,1:T(8,128)}, u32[]{:S(2)}) copy-start(f32[4096,64]{0,1:T(8,128)} %all-reduce.23.cloned.1.call-done) | copy-start | bytes 3145732
  343.4 92.1 %all-reduce.29.cloned.1.call-start = ((), (), s32[]{:S(2)}) async-start(), calls=%async_computation.6 | async-start | bytes 524288 | tf_op jit(solution)/shard_map/psum | solution.py:42
  404.1 131.7 %all-reduce.31.cloned.1.call-start = ((), (), s32[]{:S(2)}) async-start(), calls=%async_computation.7 | async-start | bytes 2097152 | tf_op jit(solution)/shard_map/psum | solution.py:68
  486.5 88.8 %all-reduce.33.cloned.1.call-start = ((), (), s32[]{:S(2)}) async-start(), calls=%async_computation.8 | async-start | bytes 524288 | tf_op jit(solution)/shard_map/psum | solution.py:42
  543.8 114.5 %all-reduce.35.cloned.1.call-start = ((), (), s32[]{:S(2)}) async-start(), calls=%async_computation.9 | async-start | bytes 2097152 | tf_op jit(solution)/shard_map/psum | solution.py:68
  600.9 57.4 %copy-start.4 = (f32[4096,64]{0,1:T(8,128)S(1)}, f32[4096,64]{0,1:T(8,128)}, u32[]{:S(2)}) copy-start(f32[4096,64]{0,1:T(8,128)} %get-tuple-element.29) | copy-start | bytes 3145732
  606.3 90.3 %all-reduce.37.cloned.1.call-start = ((), (), s32[]{:S(2)}) async-start(), calls=%async_computation.10 | async-start | bytes 524288 | tf_op jit(solution)/shard_map/psum | solution.py:42
  665.1 129.8 %all-reduce.39.cloned.1.call-start = ((), (), s32[]{:S(2)}) async-start(), calls=%async_computation.11 | async-start | bytes 2097152 | tf_op jit(solution)/shard_map/psum | solution.py:68
  740.2 54.6 %copy-start.5 = (f32[4096,64]{0,1:T(8,128)S(1)}, f32[4096,64]{0,1:T(8,128)}, u32[]{:S(2)}) copy-start(f32[4096,64]{0,1:T(8,128)} %get-tuple-element.29) | copy-start | bytes 3145732
  745.6 87.6 %all-reduce.41.cloned.1.call-start = ((), (), s32[]{:S(2)}) async-start(), calls=%async_computation.12 | async-start | bytes 524288 | tf_op jit(solution)/shard_map/psum | solution.py:42
  796.2 38.6 %copy-start.1 = (s32[4096]{0:T(1024)S(1)}, s32[4096]{0:T(1024)}, u32[]{:S(2)}) copy-start(s32[4096]{0:T(1024)} %param.8) | copy-start | bytes 49156
Sparse Core Ops, SparseCore 0:
  15.1 34.6 all-reduce.16
  80.9 51.8 all-reduce.18
  141.5 31.3 all-reduce.20
  221.1 49.1 all-reduce.22
  279.0 31.3 all-reduce.24
  343.5 51.8 all-reduce.26
  404.2 31.3 all-reduce.28
  486.6 49.1 all-reduce.30
  543.9 31.3 all-reduce.32
  606.4 51.8 all-reduce.34
  665.2 31.3 all-reduce.36
  745.8 49.0 all-reduce.38
  801.8 31.3 all-reduce.40
where the time goes:
time: 851 us; the launch traced here: 842 us
  waiting for transfers between devices  517 us (61%)
  local copies, waits for them, and re-layouts  136 us (16%)
  matrix products  98.5 us (12%)
  other arithmetic  38.8 us (5%)
  blocking collectives  35.3 us (4%)
  between operations  14.8 us (2%)
    psum x6, waiting for transfers between devices, advance(): grad_total = lax.psum(grad_local, 'samp')  297 us
    psum x7, waiting for transfers between devices, total_logits(): summed = lax.psum(partial_sum, 'feat')  220 us
    reshape x6, local copies, waits for them, and re-layouts, evaluate(): grad_tiles = grad_tiles.reshape(blocks_here * per_row, block_size * classes)  47.3 us
    dot_general x6, local copies, waits for them, and re-layouts, evaluate(): jnp.einsum('rbij,ric->rbjc', x_rows, dz_blocks, preferred_element_type=jn...  41.4 us
    psum x3, blocking collectives, evaluate(): loss = lax.psum(local_loss, 'samp') / counts  35.3 us
    reshape x12, local copies, waits for them, and re-layouts, evaluate(): return (loss, grad_local.reshape(feat_rows, classes))  34.1 us
    dot_general x7, matrix products, total_logits(): jnp.einsum('rbij,rbjc->ric', x_rows, tiles, preferred_element_type=jnp.fl...  32.2 us
    dot_general x6, matrix products, evaluate(): jnp.einsum('rbij,ric->rbjc', x_rows, dz_blocks, preferred_element_type=jn...  29.8 us
  transfers between devices with their start and end apart: 13, of which 13 were waited for; matrix products, arithmetic and copies ran while one was open for 1% of the time, Pallas kernels for 0%

commit v1 on v0

v1 whole, which is shorter than its diff:
```python
import functools

import jax
import jax.numpy as jnp
from jax import lax
from jax.experimental import pallas as pl
from jax.experimental.pallas import tpu as pltpu
from jax.sharding import PartitionSpec as P

GRP = 8
STEPS = 3
LEND = 2
LANES = 128
CUTS = (64,)

weight_rate = 8.0
adv_rate = 2.0

F32 = jnp.float32
BF16 = jnp.bfloat16
VM = pl.BlockSpec(memory_space=pltpu.VMEM)
SM = pl.BlockSpec(memory_space=pltpu.SMEM)
HBM = pl.BlockSpec(memory_space=pltpu.HBM)
PARAMS = pltpu.CompilerParams(vmem_limit_bytes=24 << 20)


def shape(dims, dtype):
    return jax.ShapeDtypeStruct(dims, dtype)


def cost(flops, bytes_accessed):
    return pl.CostEstimate(flops=flops, bytes_accessed=bytes_accessed, transcendentals=0)


def lane_sum(rows):
    return jnp.broadcast_to(jnp.sum(rows, axis=1, keepdims=True), rows.shape)


def tree_sum(parts):
    while len(parts) > 1:
        parts = [a + b for a, b in zip(parts[::2], parts[1::2], strict=True)]
    return parts[0]


def group_hot(row):
    return (lax.broadcasted_iota(jnp.int32, (GRP, LANES), 0) == row).astype(F32)


def row_data(x_ref, row):
    return jnp.concatenate([x_ref[row, j] for j in range(x_ref.shape[1])], axis=1)


def setup_kernel(
    sel, row_blocks, bounds, me_ref, picks_hbm, cols_hbm, gid_hbm, w_hbm, x_hbm, slots_ref, live_ref, counts_ref, xv_ref,
    *refs
):
    chunks = len(bounds)
    owns, zs = refs[:chunks], refs[chunks : 2 * chunks]
    wall, picks_ref, cols_ref, gid_ref, w_ref, sems = refs[2 * chunks :]

    def fetch(source, target, place):
        copy = pltpu.make_async_copy(source, target, sems.at[place])
        copy.start()
        return copy

    get_picks = fetch(picks_hbm, picks_ref, 0)
    get_w = fetch(w_hbm, w_ref, 1)
    get_cols = fetch(cols_hbm, cols_ref, 2)
    get_gid = fetch(gid_hbm, gid_ref, 3)
    get_rows = [fetch(x_hbm.at[row], xv_ref.at[row], 4 + row) for row in range(row_blocks)]
    slots = slots_ref.shape[1]
    me = me_ref[0]
    samp_count = picks_ref.shape[1] // sel
    before = lax.rem(me + samp_count - 1, samp_count)
    for step in range(STEPS):
        for slot in range(slots):
            slots_ref[step, slot] = 0
            live_ref[step, slot] = 0
    get_picks.wait()
    for step in range(STEPS):
        found = jnp.int32(0)
        for start in (me * sel, before * sel):
            for entry in range(sel):
                block = picks_ref[step, start + entry]
                mine = (block // row_blocks) == me
                place = jnp.minimum(found, slots - 1)

                @pl.when(mine)
                def _(step=step, place=place, block=block):
                    slots_ref[step, place] = block - me * row_blocks
                    live_ref[step, place] = 1

                found = found + mine.astype(jnp.int32)
    get_w.wait()
    for col in range(wall.shape[0]):
        wall[col] = w_ref[:, col * LANES : (col + 1) * LANES].astype(BF16)
    size = owns[0].shape[0]
    for col in range(size):
        start = pl.multiple_of((me * size + col) * LANES, LANES)
        for own, (low, high) in zip(owns, bounds, strict=True):
            own[col] = w_ref[low:high, pl.ds(start, LANES)]
    get_gid.wait()
    for step in range(STEPS):

        def count(entry, total, step=step):
            return total + group_hot(gid_ref[pl.ds(picks_ref[step, entry], 1), :])

        total = lax.fori_loop(0, picks_ref.shape[1], count, jnp.zeros((GRP, LANES), F32))
        counts_ref[step] = lane_sum(total)
    get_cols.wait()
    for copy in get_rows:
        copy.wait()
    for slot in range(slots):
        row = slots_ref[0, slot]
        tiles = jnp.concatenate([wall[cols_ref[j, me * row_blocks + row]] for j in range(xv_ref.shape[1])], axis=1)
        piece = lax.dot_general(
            tiles, row_data(xv_ref, row), (((1,), (1,)), ((), ())), preferred_element_type=F32
        )
        for z, (low, high) in zip(zs, bounds, strict=True):
            z[slot] = piece[low:high]


def flip_kernel(x_ref, out_ref):
    for row in range(x_ref.shape[0]):
        for j in range(x_ref.shape[1]):
            out_ref[row, j] = x_ref[row, j].T


def forward_kernel(step, row_blocks, me_ref, slots_ref, cols_ref, xt_ref, *refs):
    parts, (z_ref, wall) = refs[:-2], refs[-2:]
    me = me_ref[0]
    per_row, depth, rows = xt_ref.shape[1:]
    if len(parts) > 1:
        size = parts[0].shape[0]
        for mask in range(len(parts)):
            start = (me ^ mask) * size
            for col in range(size):
                wall[start + col] = parts[mask][col]
        weights = wall
    else:
        weights = parts[0]
    for slot in range(z_ref.shape[0]):
        row = slot if step is None else slots_ref[step, slot]
        tiles = jnp.concatenate([weights[cols_ref[j, me * row_blocks + row]] for j in range(per_row)], axis=1)
        z_ref[slot] = jnp.dot(tiles, xt_ref[row].reshape(per_row * depth, rows), preferred_element_type=F32)


def send_out(n_samp, me, acc, own_ref, sends, tail):
    size, classes, _ = own_ref.shape
    rows = size * classes
    for col in range(size):
        own_ref[col] = acc[me * size + col]
    if len(sends) == 1:
        for owner in range(n_samp):
            for col in range(size):
                sends[0][owner, col * classes : (col + 1) * classes, :] = acc[owner * size + col].astype(
                    sends[0].dtype
                )
            if tail is not None:
                sends[0][owner, rows : rows + tail.shape[0], :] = tail
        return
    for mask in range(1, n_samp):
        send = sends[mask - 1]
        start = (me ^ mask) * size
        for col in range(size):
            send[col * classes : (col + 1) * classes, :] = acc[start + col].astype(send.dtype)
        if tail is not None:
            send[rows : rows + tail.shape[0], :] = tail


def add_pieces(acc, cols_ref, row, piece):
    for j in range(cols_ref.shape[0]):
        col = cols_ref[j, row]
        acc[col] = acc[col] + piece[:, j * LANES : (j + 1) * LANES]


def grad_kernel(
    step, n_samp, row_blocks, bounds, me_ref, slots_ref, live_ref, cols_ref, x_ref, label_ref, gid_ref, q_ref, counts_ref,
    *refs
):
    chunks = len(bounds)
    halves, refs = refs[: 2 * chunks], refs[2 * chunks :]
    (own_ref, loss_ref), rests, refs = refs[:2], refs[2 : 1 + chunks], refs[1 + chunks :]
    sends, acc = refs[:-1], refs[-1]
    me = me_ref[0]
    acc[...] = jnp.zeros_like(acc)
    classes = bounds[-1][1]
    weight = q_ref[...] / counts_ref[step]
    loss = jnp.zeros((GRP, LANES), F32)
    for slot in range(slots_ref.shape[1]):
        local = slots_ref[step, slot]
        row = me * row_blocks + local
        mult = live_ref[step, slot].astype(F32)
        logits = jnp.concatenate([halves[2 * h][slot] + halves[2 * h + 1][slot] for h in range(chunks)], axis=0)
        hot = (
            lax.broadcasted_iota(jnp.int32, (classes, LANES), 0) == label_ref[pl.ds(row, 1), :]
        ).astype(F32)
        groups = group_hot(gid_ref[pl.ds(row, 1), :])
        top = jnp.max(logits, axis=0, keepdims=True)
        log_total = top + jnp.log(jnp.sum(jnp.exp(logits - top), axis=0, keepdims=True))
        cross = log_total - jnp.sum(logits * hot, axis=0, keepdims=True)
        probs = jnp.exp(logits - log_total)
        loss = loss + groups * (mult * cross)
        coef = jnp.sum(groups * weight, axis=0, keepdims=True) * mult
        dz = (coef * (probs - hot)).astype(BF16)
        for rest, (low, high) in zip(rests, bounds[1:], strict=True):
            rest[slot] = dz[low:high]
        piece = jnp.dot(dz[: bounds[0][1]], row_data(x_ref, local), preferred_element_type=F32)
        add_pieces(acc, cols_ref, row, piece)
    loss = lane_sum(loss)
    loss_ref[...] = loss
    tail = loss
    if sends[0].dtype == BF16:
        high = loss.astype(BF16).astype(F32)
        rest = loss - high
        middle = rest.astype(BF16).astype(F32)
        low = rest - middle
        left = lax.broadcasted_iota(jnp.int32, (GRP, LANES), 1) < LANES // 2
        tail = jnp.concatenate([jnp.where(left, high, low), middle], axis=0).astype(BF16)
    send_out(n_samp, me, acc, own_ref, sends, tail)


def more_grad_kernel(step, n_samp, row_blocks, me_ref, slots_ref, cols_ref, x_ref, dz_ref, own_ref, *refs):
    sends, acc = refs[:-1], refs[-1]
    me = me_ref[0]
    acc[...] = jnp.zeros_like(acc)
    for slot in range(slots_ref.shape[1]):
        local = slots_ref[step, slot]
        piece = jnp.dot(dz_ref[slot], row_data(x_ref, local), preferred_element_type=F32)
        add_pieces(acc, cols_ref, me * row_blocks + local, piece)
    send_out(n_samp, me, acc, own_ref, sends, None)


def new_weights(rate, me_ref, own_ref, w_ref, recvs, w_out, wbf_out):
    size, classes, _ = own_ref.shape
    for col in range(size):
        span = slice(col * classes, (col + 1) * classes)
        own = own_ref[col]
        if len(recvs) == 1:
            parts = [
                jnp.where(me_ref[0] == i, own, recvs[0][i, span, :].astype(F32)) for i in range(recvs[0].shape[0])
            ]
        else:
            parts = [own] + [recv[span, :].astype(F32) for recv in recvs]
        state = w_ref[col] - rate * tree_sum(parts)
        if w_out is not None:
            w_out[col] = state
        wbf_out[col] = state.astype(BF16)


def update_kernel(step, rate, keep, count, me_ref, own_ref, w_ref, loss_ref, q_ref, counts_ref, *refs):
    recvs, outs = list(refs[:count])[::-1], list(refs[count:])
    size, classes, _ = own_ref.shape
    rows = size * classes
    more = 2 * GRP if recvs[0].dtype == BF16 else GRP

    def loss_of(tail):
        if tail.dtype == F32:
            return tail[:, :1]
        tail = tail.astype(F32)
        return (tail[:GRP, :1] + tail[GRP:, :1]) + tail[:GRP, LANES // 2 : LANES // 2 + 1]

    if len(recvs) == 1:
        loss = tree_sum([loss_of(recvs[0][i, rows : rows + more, :]) for i in range(recvs[0].shape[0])])
    else:
        loss = tree_sum([loss_ref[:, :1]] + [loss_of(recv[rows : rows + more, :]) for recv in recvs])
    score = jnp.log(q_ref[...]) + adv_rate * (loss / counts_ref[step])
    grown = jnp.exp(score - jnp.max(score, axis=0, keepdims=True))
    outs[0][...] = grown / jnp.sum(grown, axis=0, keepdims=True)
    new_weights(rate, me_ref, own_ref, w_ref, recvs, outs[2] if keep else None, outs[1])


def more_update_kernel(rate, keep, count, me_ref, own_ref, w_ref, *refs):
    recvs, outs = list(refs[:count])[::-1], list(refs[count:])
    new_weights(rate, me_ref, own_ref, w_ref, recvs, outs[1] if keep else None, outs[0])


def scores_kernel(bounds, *refs):
    out_ref = refs[-1]
    for h, (low, high) in enumerate(bounds):
        for block in range(refs[0].shape[0]):
            out_ref[low:high, block * LANES : (block + 1) * LANES] = refs[2 * h][block] + refs[2 * h + 1][block]


def swap(value, axis, mask):
    count = lax.axis_size(axis)
    return lax.ppermute(value, axis, [(i, i ^ mask) for i in range(count)])


def swaps(values, axis):
    count = len(values) + 1
    order = sorted(range(1, count), key=lambda mask: (mask < count // 2, mask))
    got = {mask: swap(values[mask - 1], axis, mask) for mask in order}
    return [got[mask] for mask in range(1, count)]


def feat_halves(partial):
    count = lax.axis_size("feat")
    mask = 1
    while mask * 2 < count:
        partial = partial + swap(partial, "feat", mask)
        mask *= 2
    return partial, swap(partial, "feat", mask)


def per_device(x_blocks, block_cols, labels, group_ids, picks, w_init):
    row_blocks, per_row, block_size, _ = x_blocks.shape
    feat_rows, classes = w_init.shape
    col_blocks = feat_rows // block_size
    total_blocks = block_cols.shape[0]
    n_samp = lax.axis_size("samp")
    n_feat = lax.axis_size("feat")
    rate = weight_rate * picks.shape[1] / (per_row * n_feat)
    sel = picks.shape[1] // n_samp
    slots = min(row_blocks, sel - 1 + LEND)
    size = col_blocks // n_samp
    direct = 2 < n_samp <= 8
    me = lax.axis_index("samp").astype(jnp.int32).reshape(1)
    label_rows = labels.reshape(total_blocks, block_size)
    gid_rows = group_ids.reshape(total_blocks, block_size)
    cols = block_cols.T
    ends = [classes * cut // 64 for cut in CUTS]
    bounds = list(zip([0] + ends[:-1], ends, strict=True))
    widths = [high - low for low, high in bounds]
    chunks = len(bounds)
    work = 2 * slots * per_row * block_size * block_size

    def blocks(count, width, dtype):
        return shape((count, width, block_size), dtype)

    slot_table, live, counts, x_data, *rest = pl.pallas_call(
        functools.partial(setup_kernel, sel, row_blocks, bounds),
        out_shape=(
            shape((STEPS, slots), jnp.int32),
            shape((STEPS, slots), jnp.int32),
            shape((STEPS, GRP, LANES), F32),
            shape(x_blocks.shape, BF16),
            *[blocks(size, width, F32) for width in widths],
            *[blocks(slots, width, F32) for width in widths],
        ),
        in_specs=[SM] + [HBM] * 5,
        out_specs=(SM, SM) + (VM,) * (2 + 2 * chunks),
        scratch_shapes=[
            pltpu.VMEM((col_blocks, classes, block_size), BF16),
            pltpu.SMEM(picks.shape, jnp.int32),
            pltpu.SMEM(cols.shape, jnp.int32),
            pltpu.VMEM(gid_rows.shape, jnp.int32),
            pltpu.VMEM((classes, feat_rows), F32),
            pltpu.SemaphoreType.DMA((4 + row_blocks,)),
        ],
        compiler_params=PARAMS,
        name="setup",
    )(me, *[pltpu.with_memory_space_constraint(each, pltpu.HBM) for each in (picks, cols, gid_rows, w_init.T, x_blocks)])
    states, partials = rest[:chunks], rest[chunks:]

    def flip(after):
        data, _ = lax.optimization_barrier((x_data, after))
        return pl.pallas_call(
            flip_kernel,
            out_shape=shape(x_blocks.shape, BF16),
            in_specs=[VM],
            out_specs=VM,
            compiler_params=PARAMS,
            cost_estimate=cost(0, 4 * x_blocks.size),
            name="flip",
        )(data)

    def forward(parts, step, width):
        count = row_blocks if step is None else slots
        return pl.pallas_call(
            functools.partial(forward_kernel, step, row_blocks),
            out_shape=blocks(count, width, F32),
            in_specs=[SM, SM, SM] + [VM] * (1 + len(parts)),
            out_specs=VM,
            scratch_shapes=[pltpu.VMEM((col_blocks, width, block_size), BF16)],
            compiler_params=PARAMS,
            cost_estimate=cost(work * width, work),
            name="forward",
        )(me, slot_table, cols, flipped[0], *parts)

    def send_shapes(rows, dtype):
        if direct:
            return (shape((rows, LANES), dtype),) * (n_samp - 1)
        return (shape((n_samp, rows, LANES), dtype),)

    def exchange(sends):
        if direct:
            return swaps(sends, "samp")
        return [lax.all_to_all(sends[0], "samp", 0, 0)]

    def collect(new_bf):
        if direct:
            return [new_bf] + swaps([new_bf] * (n_samp - 1), "samp")
        return [lax.all_gather(new_bf, "samp", axis=0, tiled=True)]

    def evaluate(halves, bases, adversary, step_q, step, keep, sent):
        sends = send_shapes(size * widths[0] + (2 * GRP if sent == BF16 else GRP), sent)
        own, loss, *rest = pl.pallas_call(
            functools.partial(grad_kernel, step, n_samp, row_blocks, bounds),
            out_shape=(
                blocks(size, widths[0], F32),
                shape((GRP, LANES), F32),
                *[blocks(slots, width, BF16) for width in widths[1:]],
                *sends,
            ),
            in_specs=[SM, SM, SM, SM] + [VM] * (5 + 2 * chunks),
            out_specs=(VM,) * (1 + chunks + len(sends)),
            scratch_shapes=[pltpu.VMEM((col_blocks, widths[0], block_size), F32)],
            compiler_params=PARAMS,
            cost_estimate=cost(work * widths[0], work),
            name="grad",
        )(me, slot_table, live, cols, x_data, label_rows, gid_rows, adversary, counts, *sum(halves, ()))
        if not flipped:
            flipped.append(flip(loss))
        rests, sends = rest[: chunks - 1], rest[chunks - 1 :]
        recvs = [exchange(sends)]
        owns = [own]
        for width, dz in zip(widths[1:], rests, strict=True):
            sends = send_shapes(size * width, sent)
            own, *sends = pl.pallas_call(
                functools.partial(more_grad_kernel, step, n_samp, row_blocks),
                out_shape=(blocks(size, width, F32), *sends),
                in_specs=[SM, SM, SM, VM, VM],
                out_specs=(VM,) * (1 + len(sends)),
                scratch_shapes=[pltpu.VMEM((col_blocks, width, block_size), F32)],
                compiler_params=PARAMS,
                cost_estimate=cost(work * width, work),
                name="more_grad",
            )(me, slot_table, cols, x_data, dz)
            owns.append(own)
            recvs.append(exchange(sends))
        news, logits = [], []
        for h, width in enumerate(widths):
            outs = (blocks(size, width, BF16),) + ((blocks(size, width, F32),) if keep else ())
            count = len(recvs[h])
            if h == 0:
                new_q, new_bf, *new = pl.pallas_call(
                    functools.partial(update_kernel, step, rate, keep, count),
                    out_shape=(shape((GRP, LANES), F32), *outs),
                    in_specs=[SM] + [VM] * (5 + count),
                    out_specs=(VM,) * (1 + len(outs)),
                    compiler_params=PARAMS,
                    name="update",
                )(me, owns[h], bases[h], loss, step_q, counts, *recvs[h][::-1])
            else:
                new_bf, *new = pl.pallas_call(
                    functools.partial(more_update_kernel, rate, keep, count),
                    out_shape=outs,
                    in_specs=[SM] + [VM] * (2 + count),
                    out_specs=(VM,) * len(outs),
                    compiler_params=PARAMS,
                    name="more_update",
                )(me, owns[h], bases[h], *recvs[h][::-1])
            news += new
            logits.append(collect(new_bf))
        return news, logits, new_q

    def halves_of(parts, step):
        return [feat_halves(forward(part, step, width)) for part, width in zip(parts, widths, strict=True)]

    flipped = []
    adversary = jnp.full((GRP, LANES), 1.0 / GRP, F32)
    halves = [feat_halves(partial) for partial in partials]
    for step in range(STEPS):
        _, parts, half_q = evaluate(halves, states, adversary, adversary, step, False, BF16 if step else F32)
        halves = halves_of(parts, step)
        states_new, parts, adversary = evaluate(halves, states, half_q, adversary, step, step + 1 < STEPS, BF16)
        if step + 1 < STEPS:
            states = states_new
            halves = halves_of(parts, step + 1)
    final = halves_of(parts, None)
    scores = pl.pallas_call(
        functools.partial(scores_kernel, bounds),
        out_shape=shape((classes, row_blocks * block_size), F32),
        in_specs=[VM] * (2 * chunks),
        out_specs=VM,
        compiler_params=PARAMS,
        name="scores",
    )(*sum(final, ()))
    return (scores.T, adversary[:, 0])


def solution(mesh):
    in_specs = (
        P(("groups", "samp"), "feat", None, None),
        P("groups", "feat"),
        P("groups"),
        P("groups"),
        P(None, "groups"),
        P("feat", None),
    )
    out_specs = (P(("groups", "samp"), None), P("groups"))
    return jax.shard_map(
        per_device, mesh=mesh, in_specs=in_specs, out_specs=out_specs, check_vma=False
    )
```

time: 851 us -> 250 us (0.29); the launches traced: 842 us -> 250 us
  waiting for transfers between devices: 517 us -> 156 us
  local copies, waits for them, and re-layouts: 136 us -> 0.64 us
  matrix products: 98.5 us -> 0 us
  starting transfers between devices: 1 us -> 66.9 us
  other arithmetic: 38.8 us -> 0.16 us
  blocking collectives: 35.3 us -> 0 us
  Pallas kernels: 0 us -> 25.5 us
  between operations: 14.8 us -> 0.86 us
    psum x13 -> x0, waiting for transfers between devices: 517 us -> none  [the longest x6 297 us: advance(): grad_total = lax.psum(grad_local, 'samp')]
    ppermute x0 -> x50, waiting for transfers between devices: none -> 156 us  [swap(): return lax.ppermute(value, axis, [(i, i ^ mask) for i in range(count)])]
    dot_general x34 -> x0, matrix products: 98.5 us -> none  [the longest x7 32.2 us: total_logits(): jnp.einsum('rbij,rbjc->ric', x_rows, tiles, preferred_element_type=jnp.fl...]
    reshape x20 -> x0, local copies, waits for them, and re-layouts: 82.3 us -> none  [the longest x6 47.3 us: evaluate(): grad_tiles = grad_tiles.reshape(blocks_here * per_row, block_size * classes)]
    ppermute x0 -> x50, starting transfers between devices: none -> 66.9 us  [swap(): return lax.ppermute(value, axis, [(i, i ^ mask) for i in range(count)])]
    dot_general x6 -> x0, local copies, waits for them, and re-layouts: 41.4 us -> none  [evaluate(): jnp.einsum('rbij,ric->rbjc', x_rows, dz_blocks, preferred_element_type=jn...]
    psum x3 -> x0, blocking collectives: 35.3 us -> none  [evaluate(): loss = lax.psum(local_loss, 'samp') / counts]
    pallas_call x0 -> x21, Pallas kernels: none -> 25.5 us  [the longest x6 9.93 us: evaluate(): pl.pallas_call(functools.partial(grad_kernel, step, n_samp, row_blocks, b...]
  transfers between devices with their start and end apart: 13 -> 50, of which waited for: 13 -> 38; matrix products, arithmetic and copies ran while one was open for 1% -> 0% of each run, Pallas kernels for 0% -> 0%
where the time goes in v1:
time: 250 us
  waiting for transfers between devices  156 us (62%)
  starting transfers between devices  66.9 us (27%)
  Pallas kernels  25.5 us (10%)
    ppermute x50, waiting for transfers between devices, swap(): return lax.ppermute(value, axis, [(i, i ^ mask) for i in range(count)])  156 us
    ppermute x50, starting transfers between devices, swap(): return lax.ppermute(value, axis, [(i, i ^ mask) for i in range(count)])  66.9 us
    pallas_call x6, Pallas kernels, evaluate(): pl.pallas_call(functools.partial(grad_kernel, step, n_samp, row_blocks, b...  9.93 us
    pallas_call x6, Pallas kernels, forward(): pl.pallas_call(functools.partial(forward_kernel, step, row_blocks), out_s...  8.64 us
  transfers between devices with their start and end apart: 50, of which 38 were waited for; matrix products, arithmetic and copies ran while one was open for 0% of the time, Pallas kernels for 0%

profile of v1, /device:TPU:0, one launch (start us, length us, event | category | flops | bytes accessed | tf_op | source)
XLA Modules:
  0.0 249.9 jit_solution(8982791055463226041)
XLA Ops:
  0.7 4.0 %setup.1 = (s32[3,5]{1,0:T(4,128)S(1)}, s32[3,5]{1,0:T(4,128)S(1)}, f32[3,8,128]{2,1,0:T(8,128)S(1)}, bf16[8,16,128,128]{3,2,1,0:T(8,128)(2,1)S(1)}, f32[8,64,12...) custom-call(s32[1]{0:T(128)} %bitcast.me_ref, s32[3,16]{1,0:T(4,128)} %picks_hbm.1, s32[16,32]{1,0:T(8,128)} %bitcast.6, ...), custom_call_target="tpu_custom_call" | custom-call | tf_op jit(solution)/shard_map/setup/pallas_call | solution.py:331
  9.2 4.5 %collective-permute-done.1.refs_1_ = f32[5,64,128]{2,1,0:T(8,128)S(1)} collective-permute-done((f32[5,64,128]{2,1,0:T(8,128)S(1)}, f32[5,64,128]{2,1,0:T(8,128)S(1)}, u32[]{:S(2)}, u32[]{:S(2)}) %collective-permute-start.1) | collective-permute-done | bytes 163872 | tf_op jit(solution)/shard_map/ppermute | solution.py:287
  15.4 3.9 %collective-permute-start.2 = (f32[520,128]{1,0:T(8,128)S(1)}, f32[520,128]{1,0:T(8,128)S(1)}, u32[]{:S(2)}, u32[]{:S(2)}) collective-permute-start(f32[520,128]{1,0:T(8,128)S(1)} %get-tuple-element.62), channel_id=1, source_target_pairs={{0,12},{4,8},{8,4},{12,0},{1,13},{5,9},{9,5},{13,1},{2,14},{6,10},... | collective-permute-start | bytes 798728 | tf_op jit(solution)/shard_map/ppermute | solution.py:287
  20.0 6.7 %collective-permute-done.2.refs_0_ = f32[520,128]{1,0:T(8,128)S(1)} collective-permute-done((f32[520,128]{1,0:T(8,128)S(1)}, f32[520,128]{1,0:T(8,128)S(1)}, u32[]{:S(2)}, u32[]{:S(2)}) %collective-permute-start.2) | collective-permute-done | bytes 266272 | tf_op jit(solution)/shard_map/ppermute | solution.py:287
  26.7 14.7 %collective-permute-done.3.refs_1_ = f32[520,128]{1,0:T(8,128)S(1)} collective-permute-done((f32[520,128]{1,0:T(8,128)S(1)}, f32[520,128]{1,0:T(8,128)S(1)}, u32[]{:S(2)}, u32[]{:S(2)}) %collective-permute-start.3) | collective-permute-done | bytes 266272 | tf_op jit(solution)/shard_map/ppermute | solution.py:287
  49.9 4.3 %collective-permute-done.6.refs_2_ = bf16[8,64,128]{2,1,0:T(8,128)(2,1)S(1)} collective-permute-done((bf16[8,64,128]{2,1,0:T(8,128)(2,1)S(1)}, bf16[8,64,128]{2,1,0:T(8,128)(2,1)S(1)}, u32[]{:S(2)}, u32[]{:S(2)}) %collective-permute-start.6) | collective-permute-done | bytes 131104 | tf_op jit(solution)/shard_map/ppermute | solution.py:287
  58.6 4.8 %collective-permute-done.9.refs_1_ = f32[5,64,128]{2,1,0:T(8,128)S(1)} collective-permute-done((f32[5,64,128]{2,1,0:T(8,128)S(1)}, f32[5,64,128]{2,1,0:T(8,128)S(1)}, u32[]{:S(2)}, u32[]{:S(2)}) %collective-permute-start.9) | collective-permute-done | bytes 163872 | tf_op jit(solution)/shard_map/ppermute | solution.py:287
  69.5 4.0 %collective-permute-done.10.refs_0_ = bf16[528,128]{1,0:T(8,128)(2,1)S(1)} collective-permute-done((bf16[528,128]{1,0:T(8,128)(2,1)S(1)}, bf16[528,128]{1,0:T(8,128)(2,1)S(1)}, u32[]{:S(2)}, u32[]{:S(2)}) %collective-permute-start.10) | collective-permute-done | bytes 135200 | tf_op jit(solution)/shard_map/ppermute | solution.py:287
  73.5 4.1 %collective-permute-done.11.refs_1_ = bf16[528,128]{1,0:T(8,128)(2,1)S(1)} collective-permute-done((bf16[528,128]{1,0:T(8,128)(2,1)S(1)}, bf16[528,128]{1,0:T(8,128)(2,1)S(1)}, u32[]{:S(2)}, u32[]{:S(2)}) %collective-permute-start.11) | collective-permute-done | bytes 135200 | tf_op jit(solution)/shard_map/ppermute | solution.py:287
  82.2 3.9 %collective-permute-done.15.refs_3_ = bf16[8,64,128]{2,1,0:T(8,128)(2,1)S(1)} collective-permute-done((bf16[8,64,128]{2,1,0:T(8,128)(2,1)S(1)}, bf16[8,64,128]{2,1,0:T(8,128)(2,1)S(1)}, u32[]{:S(2)}, u32[]{:S(2)}) %collective-permute-start.15) | collective-permute-done | bytes 131104 | tf_op jit(solution)/shard_map/ppermute | solution.py:287
  86.1 4.7 %collective-permute-done.14.refs_2_ = bf16[8,64,128]{2,1,0:T(8,128)(2,1)S(1)} collective-permute-done((bf16[8,64,128]{2,1,0:T(8,128)(2,1)S(1)}, bf16[8,64,128]{2,1,0:T(8,128)(2,1)S(1)}, u32[]{:S(2)}, u32[]{:S(2)}) %collective-permute-start.14) | collective-permute-done | bytes 131104 | tf_op jit(solution)/shard_map/ppermute | solution.py:287
  95.2 4.7 %collective-permute-done.17.refs_1_ = f32[5,64,128]{2,1,0:T(8,128)S(1)} collective-permute-done((f32[5,64,128]{2,1,0:T(8,128)S(1)}, f32[5,64,128]{2,1,0:T(8,128)S(1)}, u32[]{:S(2)}, u32[]{:S(2)}) %collective-permute-start.17) | collective-permute-done | bytes 163872 | tf_op jit(solution)/shard_map/ppermute | solution.py:287
  106.1 3.9 %collective-permute-done.18.refs_0_ = bf16[528,128]{1,0:T(8,128)(2,1)S(1)} collective-permute-done((bf16[528,128]{1,0:T(8,128)(2,1)S(1)}, bf16[528,128]{1,0:T(8,128)(2,1)S(1)}, u32[]{:S(2)}, u32[]{:S(2)}) %collective-permute-start.18) | collective-permute-done | bytes 135200 | tf_op jit(solution)/shard_map/ppermute | solution.py:287
  110.0 4.4 %collective-permute-done.19.refs_1_ = bf16[528,128]{1,0:T(8,128)(2,1)S(1)} collective-permute-done((bf16[528,128]{1,0:T(8,128)(2,1)S(1)}, bf16[528,128]{1,0:T(8,128)(2,1)S(1)}, u32[]{:S(2)}, u32[]{:S(2)}) %collective-permute-start.19) | collective-permute-done | bytes 135200 | tf_op jit(solution)/shard_map/ppermute | solution.py:287
  119.1 3.9 %collective-permute-done.23.refs_3_ = bf16[8,64,128]{2,1,0:T(8,128)(2,1)S(1)} collective-permute-done((bf16[8,64,128]{2,1,0:T(8,128)(2,1)S(1)}, bf16[8,64,128]{2,1,0:T(8,128)(2,1)S(1)}, u32[]{:S(2)}, u32[]{:S(2)}) %collective-permute-start.23) | collective-permute-done | bytes 131104 | tf_op jit(solution)/shard_map/ppermute | solution.py:287
  122.9 4.5 %collective-permute-done.22.refs_2_ = bf16[8,64,128]{2,1,0:T(8,128)(2,1)S(1)} collective-permute-done((bf16[8,64,128]{2,1,0:T(8,128)(2,1)S(1)}, bf16[8,64,128]{2,1,0:T(8,128)(2,1)S(1)}, u32[]{:S(2)}, u32[]{:S(2)}) %collective-permute-start.22) | collective-permute-done | bytes 131104 | tf_op jit(solution)/shard_map/ppermute | solution.py:287
  131.9 4.7 %collective-permute-done.25.refs_1_ = f32[5,64,128]{2,1,0:T(8,128)S(1)} collective-permute-done((f32[5,64,128]{2,1,0:T(8,128)S(1)}, f32[5,64,128]{2,1,0:T(8,128)S(1)}, u32[]{:S(2)}, u32[]{:S(2)}) %collective-permute-start.25) | collective-permute-done | bytes 163872 | tf_op jit(solution)/shard_map/ppermute | solution.py:287
  142.7 3.9 %collective-permute-done.26.refs_0_ = bf16[528,128]{1,0:T(8,128)(2,1)S(1)} collective-permute-done((bf16[528,128]{1,0:T(8,128)(2,1)S(1)}, bf16[528,128]{1,0:T(8,128)(2,1)S(1)}, u32[]{:S(2)}, u32[]{:S(2)}) %collective-permute-start.26) | collective-permute-done | bytes 135200 | tf_op jit(solution)/shard_map/ppermute | solution.py:287
  146.7 4.9 %collective-permute-done.27.refs_1_ = bf16[528,128]{1,0:T(8,128)(2,1)S(1)} collective-permute-done((bf16[528,128]{1,0:T(8,128)(2,1)S(1)}, bf16[528,128]{1,0:T(8,128)(2,1)S(1)}, u32[]{:S(2)}, u32[]{:S(2)}) %collective-permute-start.27) | collective-permute-done | bytes 135200 | tf_op jit(solution)/shard_map/ppermute | solution.py:287
  156.2 3.9 %collective-permute-done.31.refs_3_ = bf16[8,64,128]{2,1,0:T(8,128)(2,1)S(1)} collective-permute-done((bf16[8,64,128]{2,1,0:T(8,128)(2,1)S(1)}, bf16[8,64,128]{2,1,0:T(8,128)(2,1)S(1)}, u32[]{:S(2)}, u32[]{:S(2)}) %collective-permute-start.31) | collective-permute-done | bytes 131104 | tf_op jit(solution)/shard_map/ppermute | solution.py:287
  160.1 4.0 %collective-permute-done.30.refs_2_ = bf16[8,64,128]{2,1,0:T(8,128)(2,1)S(1)} collective-permute-done((bf16[8,64,128]{2,1,0:T(8,128)(2,1)S(1)}, bf16[8,64,128]{2,1,0:T(8,128)(2,1)S(1)}, u32[]{:S(2)}, u32[]{:S(2)}) %collective-permute-start.30) | collective-permute-done | bytes 131104 | tf_op jit(solution)/shard_map/ppermute | solution.py:287
  168.5 4.7 %collective-permute-done.33.refs_1_ = f32[5,64,128]{2,1,0:T(8,128)S(1)} collective-permute-done((f32[5,64,128]{2,1,0:T(8,128)S(1)}, f32[5,64,128]{2,1,0:T(8,128)S(1)}, u32[]{:S(2)}, u32[]{:S(2)}) %collective-permute-start.33) | collective-permute-done | bytes 163872 | tf_op jit(solution)/shard_map/ppermute | solution.py:287
  179.4 3.9 %collective-permute-done.34.refs_0_ = bf16[528,128]{1,0:T(8,128)(2,1)S(1)} collective-permute-done((bf16[528,128]{1,0:T(8,128)(2,1)S(1)}, bf16[528,128]{1,0:T(8,128)(2,1)S(1)}, u32[]{:S(2)}, u32[]{:S(2)}) %collective-permute-start.34) | collective-permute-done | bytes 135200 | tf_op jit(solution)/shard_map/ppermute | solution.py:287
  183.3 4.9 %collective-permute-done.35.refs_1_ = bf16[528,128]{1,0:T(8,128)(2,1)S(1)} collective-permute-done((bf16[528,128]{1,0:T(8,128)(2,1)S(1)}, bf16[528,128]{1,0:T(8,128)(2,1)S(1)}, u32[]{:S(2)}, u32[]{:S(2)}) %collective-permute-start.35) | collective-permute-done | bytes 135200 | tf_op jit(solution)/shard_map/ppermute | solution.py:287
  192.8 3.9 %collective-permute-done.39.refs_3_ = bf16[8,64,128]{2,1,0:T(8,128)(2,1)S(1)} collective-permute-done((bf16[8,64,128]{2,1,0:T(8,128)(2,1)S(1)}, bf16[8,64,128]{2,1,0:T(8,128)(2,1)S(1)}, u32[]{:S(2)}, u32[]{:S(2)}) %collective-permute-start.39) | collective-permute-done | bytes 131104 | tf_op jit(solution)/shard_map/ppermute | solution.py:287
  196.7 4.0 %collective-permute-done.38.refs_2_ = bf16[8,64,128]{2,1,0:T(8,128)(2,1)S(1)} collective-permute-done((bf16[8,64,128]{2,1,0:T(8,128)(2,1)S(1)}, bf16[8,64,128]{2,1,0:T(8,128)(2,1)S(1)}, u32[]{:S(2)}, u32[]{:S(2)}) %collective-permute-start.38) | collective-permute-done | bytes 131104 | tf_op jit(solution)/shard_map/ppermute | solution.py:287
  205.3 4.7 %collective-permute-done.41.refs_1_ = f32[5,64,128]{2,1,0:T(8,128)S(1)} collective-permute-done((f32[5,64,128]{2,1,0:T(8,128)S(1)}, f32[5,64,128]{2,1,0:T(8,128)S(1)}, u32[]{:S(2)}, u32[]{:S(2)}) %collective-permute-start.41) | collective-permute-done | bytes 163872 | tf_op jit(solution)/shard_map/ppermute | solution.py:287
  216.2 3.9 %collective-permute-done.42.refs_0_ = bf16[528,128]{1,0:T(8,128)(2,1)S(1)} collective-permute-done((bf16[528,128]{1,0:T(8,128)(2,1)S(1)}, bf16[528,128]{1,0:T(8,128)(2,1)S(1)}, u32[]{:S(2)}, u32[]{:S(2)}) %collective-permute-start.42) | collective-permute-done | bytes 135200 | tf_op jit(solution)/shard_map/ppermute | solution.py:287
  220.1 4.9 %collective-permute-done.43.refs_1_ = bf16[528,128]{1,0:T(8,128)(2,1)S(1)} collective-permute-done((bf16[528,128]{1,0:T(8,128)(2,1)S(1)}, bf16[528,128]{1,0:T(8,128)(2,1)S(1)}, u32[]{:S(2)}, u32[]{:S(2)}) %collective-permute-start.43) | collective-permute-done | bytes 135200 | tf_op jit(solution)/shard_map/ppermute | solution.py:287
  229.6 3.9 %collective-permute-done.47.refs_3_ = bf16[8,64,128]{2,1,0:T(8,128)(2,1)S(1)} collective-permute-done((bf16[8,64,128]{2,1,0:T(8,128)(2,1)S(1)}, bf16[8,64,128]{2,1,0:T(8,128)(2,1)S(1)}, u32[]{:S(2)}, u32[]{:S(2)}) %collective-permute-start.47) | collective-permute-done | bytes 131104 | tf_op jit(solution)/shard_map/ppermute | solution.py:287
  233.5 4.0 %collective-permute-done.46.refs_2_ = bf16[8,64,128]{2,1,0:T(8,128)(2,1)S(1)} collective-permute-done((bf16[8,64,128]{2,1,0:T(8,128)(2,1)S(1)}, bf16[8,64,128]{2,1,0:T(8,128)(2,1)S(1)}, u32[]{:S(2)}, u32[]{:S(2)}) %collective-permute-start.46) | collective-permute-done | bytes 131104 | tf_op jit(solution)/shard_map/ppermute | solution.py:287
  243.0 6.2 %collective-permute-done.49.refs_1_ = f32[8,64,128]{2,1,0:T(8,128)S(1)} collective-permute-done((f32[8,64,128]{2,1,0:T(8,128)S(1)}, f32[8,64,128]{2,1,0:T(8,128)S(1)}, u32[]{:S(2)}, u32[]{:S(2)}) %collective-permute-start.49) | collective-permute-done | bytes 262176 | tf_op jit(solution)/shard_map/ppermute | solution.py:287
  (104 shorter events, 97.5 us)
Async XLA Ops:
  15.4 11.3 %collective-permute-start.2 = (f32[520,128]{1,0:T(8,128)S(1)}, f32[520,128]{1,0:T(8,128)S(1)}, u32[]{:S(2)}, u32[]{:S(2)}) collective-permute-start(f32[520,128]{1,0:T(8,128)S(1)} %get-tuple-element.62), channel_id=1, source_target_pairs={{0,12},{4,8},{8,4},{12,0},{1,13},{5,9},{9,5},{13,1},{2,14},{6,10},... | collective-permute-start | bytes 798728 | tf_op jit(solution)/shard_map/ppermute | solution.py:287
  19.3 22.1 %collective-permute-start.3 = (f32[520,128]{1,0:T(8,128)S(1)}, f32[520,128]{1,0:T(8,128)S(1)}, u32[]{:S(2)}, u32[]{:S(2)}) collective-permute-start(f32[520,128]{1,0:T(8,128)S(1)} %get-tuple-element.63), channel_id=1, source_target_pairs={{0,8},{4,12},{8,0},{12,4},{1,9},{5,13},{9,1},{13,5},{2,10},{6,14},... | collective-permute-start | bytes 798728 | tf_op jit(solution)/shard_map/ppermute | solution.py:287
  19.3 22.1 %collective-permute-start.4 = (f32[520,128]{1,0:T(8,128)S(1)}, f32[520,128]{1,0:T(8,128)S(1)}, u32[]{:S(2)}, u32[]{:S(2)}) collective-permute-start(f32[520,128]{1,0:T(8,128)S(1)} %get-tuple-element.64), channel_id=1, source_target_pairs={{0,4},{4,0},{8,12},{12,8},{1,5},{5,1},{9,13},{13,9},{2,6},{6,2},{1... | collective-permute-start | bytes 798728 | tf_op jit(solution)/shard_map/ppermute | solution.py:287
  44.2 10.0 %collective-permute-start.6 = (bf16[8,64,128]{2,1,0:T(8,128)(2,1)S(1)}, bf16[8,64,128]{2,1,0:T(8,128)(2,1)S(1)}, u32[]{:S(2)}, u32[]{:S(2)}) collective-permute-start(bf16[8,64,128]{2,1,0:T(8,128)(2,1)S(1)} %get-tuple-element.66.refs_0_), channel_id=1, source_target_pairs={{0,8},{4,12},{8,0},{12,4},{1,9},{5,13},{9,1},{13,5},{2,10},{6,14},... | collective-permute-start | bytes 393224 | tf_op jit(solution)/shard_map/ppermute | solution.py:287
  44.2 10.0 %collective-permute-start.5 = (bf16[8,64,128]{2,1,0:T(8,128)(2,1)S(1)}, bf16[8,64,128]{2,1,0:T(8,128)(2,1)S(1)}, u32[]{:S(2)}, u32[]{:S(2)}) collective-permute-start(bf16[8,64,128]{2,1,0:T(8,128)(2,1)S(1)} %get-tuple-element.66.refs_0_), channel_id=1, source_target_pairs={{0,4},{4,0},{8,12},{12,8},{1,5},{5,1},{9,13},{13,9},{2,6},{6,2},{1... | collective-permute-start | bytes 393224 | tf_op jit(solution)/shard_map/ppermute | solution.py:287
  65.0 8.4 %collective-permute-start.10 = (bf16[528,128]{1,0:T(8,128)(2,1)S(1)}, bf16[528,128]{1,0:T(8,128)(2,1)S(1)}, u32[]{:S(2)}, u32[]{:S(2)}) collective-permute-start(bf16[528,128]{1,0:T(8,128)(2,1)S(1)} %get-tuple-element.69), channel_id=1, source_target_pairs={{0,12},{4,8},{8,4},{12,0},{1,13},{5,9},{9,5},{13,1},{2,14},{6,10},... | collective-permute-start | bytes 405512 | tf_op jit(solution)/shard_map/ppermute | solution.py:287
  66.4 11.2 %collective-permute-start.11 = (bf16[528,128]{1,0:T(8,128)(2,1)S(1)}, bf16[528,128]{1,0:T(8,128)(2,1)S(1)}, u32[]{:S(2)}, u32[]{:S(2)}) collective-permute-start(bf16[528,128]{1,0:T(8,128)(2,1)S(1)} %get-tuple-element.70), channel_id=1, source_target_pairs={{0,8},{4,12},{8,0},{12,4},{1,9},{5,13},{9,1},{13,5},{2,10},{6,14},... | collective-permute-start | bytes 405512 | tf_op jit(solution)/shard_map/ppermute | solution.py:287
  66.4 11.2 %collective-permute-start.12 = (bf16[528,128]{1,0:T(8,128)(2,1)S(1)}, bf16[528,128]{1,0:T(8,128)(2,1)S(1)}, u32[]{:S(2)}, u32[]{:S(2)}) collective-permute-start(bf16[528,128]{1,0:T(8,128)(2,1)S(1)} %get-tuple-element.71), channel_id=1, source_target_pairs={{0,4},{4,0},{8,12},{12,8},{1,5},{5,1},{9,13},{13,9},{2,6},{6,2},{1... | collective-permute-start | bytes 405512 | tf_op jit(solution)/shard_map/ppermute | solution.py:287
  79.9 10.9 %collective-permute-start.14 = (bf16[8,64,128]{2,1,0:T(8,128)(2,1)S(1)}, bf16[8,64,128]{2,1,0:T(8,128)(2,1)S(1)}, u32[]{:S(2)}, u32[]{:S(2)}) collective-permute-start(bf16[8,64,128]{2,1,0:T(8,128)(2,1)S(1)} %get-tuple-element.73.refs_0_), channel_id=1, source_target_pairs={{0,8},{4,12},{8,0},{12,4},{1,9},{5,13},{9,1},{13,5},{2,10},{6,14},... | collective-permute-start | bytes 393224 | tf_op jit(solution)/shard_map/ppermute | solution.py:287
  79.9 10.9 %collective-permute-start.13 = (bf16[8,64,128]{2,1,0:T(8,128)(2,1)S(1)}, bf16[8,64,128]{2,1,0:T(8,128)(2,1)S(1)}, u32[]{:S(2)}, u32[]{:S(2)}) collective-permute-start(bf16[8,64,128]{2,1,0:T(8,128)(2,1)S(1)} %get-tuple-element.73.refs_0_), channel_id=1, source_target_pairs={{0,4},{4,0},{8,12},{12,8},{1,5},{5,1},{9,13},{13,9},{2,6},{6,2},{1... | collective-permute-start | bytes 393224 | tf_op jit(solution)/shard_map/ppermute | solution.py:287
  101.6 8.4 %collective-permute-start.18 = (bf16[528,128]{1,0:T(8,128)(2,1)S(1)}, bf16[528,128]{1,0:T(8,128)(2,1)S(1)}, u32[]{:S(2)}, u32[]{:S(2)}) collective-permute-start(bf16[528,128]{1,0:T(8,128)(2,1)S(1)} %get-tuple-element.77), channel_id=1, source_target_pairs={{0,12},{4,8},{8,4},{12,0},{1,13},{5,9},{9,5},{13,1},{2,14},{6,10},... | collective-permute-start | bytes 405512 | tf_op jit(solution)/shard_map/ppermute | solution.py:287
  103.5 10.9 %collective-permute-start.19 = (bf16[528,128]{1,0:T(8,128)(2,1)S(1)}, bf16[528,128]{1,0:T(8,128)(2,1)S(1)}, u32[]{:S(2)}, u32[]{:S(2)}) collective-permute-start(bf16[528,128]{1,0:T(8,128)(2,1)S(1)} %get-tuple-element.78), channel_id=1, source_target_pairs={{0,8},{4,12},{8,0},{12,4},{1,9},{5,13},{9,1},{13,5},{2,10},{6,14},... | collective-permute-start | bytes 405512 | tf_op jit(solution)/shard_map/ppermute | solution.py:287
  103.5 10.9 %collective-permute-start.20 = (bf16[528,128]{1,0:T(8,128)(2,1)S(1)}, bf16[528,128]{1,0:T(8,128)(2,1)S(1)}, u32[]{:S(2)}, u32[]{:S(2)}) collective-permute-start(bf16[528,128]{1,0:T(8,128)(2,1)S(1)} %get-tuple-element.79), channel_id=1, source_target_pairs={{0,4},{4,0},{8,12},{12,8},{1,5},{5,1},{9,13},{13,9},{2,6},{6,2},{1... | collective-permute-start | bytes 405512 | tf_op jit(solution)/shard_map/ppermute | solution.py:287
  117.1 10.3 %collective-permute-start.22 = (bf16[8,64,128]{2,1,0:T(8,128)(2,1)S(1)}, bf16[8,64,128]{2,1,0:T(8,128)(2,1)S(1)}, u32[]{:S(2)}, u32[]{:S(2)}) collective-permute-start(bf16[8,64,128]{2,1,0:T(8,128)(2,1)S(1)} %get-tuple-element.81.refs_0_), channel_id=1, source_target_pairs={{0,8},{4,12},{8,0},{12,4},{1,9},{5,13},{9,1},{13,5},{2,10},{6,14},... | collective-permute-start | bytes 393224 | tf_op jit(solution)/shard_map/ppermute | solution.py:287
  117.1 10.3 %collective-permute-start.21 = (bf16[8,64,128]{2,1,0:T(8,128)(2,1)S(1)}, bf16[8,64,128]{2,1,0:T(8,128)(2,1)S(1)}, u32[]{:S(2)}, u32[]{:S(2)}) collective-permute-start(bf16[8,64,128]{2,1,0:T(8,128)(2,1)S(1)} %get-tuple-element.81.refs_0_), channel_id=1, source_target_pairs={{0,4},{4,0},{8,12},{12,8},{1,5},{5,1},{9,13},{13,9},{2,6},{6,2},{1... | collective-permute-start | bytes 393224 | tf_op jit(solution)/shard_map/ppermute | solution.py:287
  138.3 8.4 %collective-permute-start.26 = (bf16[528,128]{1,0:T(8,128)(2,1)S(1)}, bf16[528,128]{1,0:T(8,128)(2,1)S(1)}, u32[]{:S(2)}, u32[]{:S(2)}) collective-permute-start(bf16[528,128]{1,0:T(8,128)(2,1)S(1)} %get-tuple-element.84), channel_id=1, source_target_pairs={{0,12},{4,8},{8,4},{12,0},{1,13},{5,9},{9,5},{13,1},{2,14},{6,10},... | collective-permute-start | bytes 405512 | tf_op jit(solution)/shard_map/ppermute | solution.py:287
  140.2 11.4 %collective-permute-start.27 = (bf16[528,128]{1,0:T(8,128)(2,1)S(1)}, bf16[528,128]{1,0:T(8,128)(2,1)S(1)}, u32[]{:S(2)}, u32[]{:S(2)}) collective-permute-start(bf16[528,128]{1,0:T(8,128)(2,1)S(1)} %get-tuple-element.85), channel_id=1, source_target_pairs={{0,8},{4,12},{8,0},{12,4},{1,9},{5,13},{9,1},{13,5},{2,10},{6,14},... | collective-permute-start | bytes 405512 | tf_op jit(solution)/shard_map/ppermute | solution.py:287
  140.2 11.4 %collective-permute-start.28 = (bf16[528,128]{1,0:T(8,128)(2,1)S(1)}, bf16[528,128]{1,0:T(8,128)(2,1)S(1)}, u32[]{:S(2)}, u32[]{:S(2)}) collective-permute-start(bf16[528,128]{1,0:T(8,128)(2,1)S(1)} %get-tuple-element.86), channel_id=1, source_target_pairs={{0,4},{4,0},{8,12},{12,8},{1,5},{5,1},{9,13},{13,9},{2,6},{6,2},{1... | collective-permute-start | bytes 405512 | tf_op jit(solution)/shard_map/ppermute | solution.py:287
  151.7 8.4 %collective-permute-start.31 = (bf16[8,64,128]{2,1,0:T(8,128)(2,1)S(1)}, bf16[8,64,128]{2,1,0:T(8,128)(2,1)S(1)}, u32[]{:S(2)}, u32[]{:S(2)}) collective-permute-start(bf16[8,64,128]{2,1,0:T(8,128)(2,1)S(1)} %get-tuple-element.88.refs_0_), channel_id=1, source_target_pairs={{0,12},{4,8},{8,4},{12,0},{1,13},{5,9},{9,5},{13,1},{2,14},{6,10},... | collective-permute-start | bytes 393224 | tf_op jit(solution)/shard_map/ppermute | solution.py:287
  153.8 10.3 %collective-permute-start.30 = (bf16[8,64,128]{2,1,0:T(8,128)(2,1)S(1)}, bf16[8,64,128]{2,1,0:T(8,128)(2,1)S(1)}, u32[]{:S(2)}, u32[]{:S(2)}) collective-permute-start(bf16[8,64,128]{2,1,0:T(8,128)(2,1)S(1)} %get-tuple-element.88.refs_0_), channel_id=1, source_target_pairs={{0,8},{4,12},{8,0},{12,4},{1,9},{5,13},{9,1},{13,5},{2,10},{6,14},... | collective-permute-start | bytes 393224 | tf_op jit(solution)/shard_map/ppermute | solution.py:287
  153.8 10.3 %collective-permute-start.29 = (bf16[8,64,128]{2,1,0:T(8,128)(2,1)S(1)}, bf16[8,64,128]{2,1,0:T(8,128)(2,1)S(1)}, u32[]{:S(2)}, u32[]{:S(2)}) collective-permute-start(bf16[8,64,128]{2,1,0:T(8,128)(2,1)S(1)} %get-tuple-element.88.refs_0_), channel_id=1, source_target_pairs={{0,4},{4,0},{8,12},{12,8},{1,5},{5,1},{9,13},{13,9},{2,6},{6,2},{1... | collective-permute-start | bytes 393224 | tf_op jit(solution)/shard_map/ppermute | solution.py:287
  174.9 8.4 %collective-permute-start.34 = (bf16[528,128]{1,0:T(8,128)(2,1)S(1)}, bf16[528,128]{1,0:T(8,128)(2,1)S(1)}, u32[]{:S(2)}, u32[]{:S(2)}) collective-permute-start(bf16[528,128]{1,0:T(8,128)(2,1)S(1)} %get-tuple-element.92), channel_id=1, source_target_pairs={{0,12},{4,8},{8,4},{12,0},{1,13},{5,9},{9,5},{13,1},{2,14},{6,10},... | collective-permute-start | bytes 405512 | tf_op jit(solution)/shard_map/ppermute | solution.py:287
  176.8 11.4 %collective-permute-start.35 = (bf16[528,128]{1,0:T(8,128)(2,1)S(1)}, bf16[528,128]{1,0:T(8,128)(2,1)S(1)}, u32[]{:S(2)}, u32[]{:S(2)}) collective-permute-start(bf16[528,128]{1,0:T(8,128)(2,1)S(1)} %get-tuple-element.93), channel_id=1, source_target_pairs={{0,8},{4,12},{8,0},{12,4},{1,9},{5,13},{9,1},{13,5},{2,10},{6,14},... | collective-permute-start | bytes 405512 | tf_op jit(solution)/shard_map/ppermute | solution.py:287
  176.8 11.4 %collective-permute-start.36 = (bf16[528,128]{1,0:T(8,128)(2,1)S(1)}, bf16[528,128]{1,0:T(8,128)(2,1)S(1)}, u32[]{:S(2)}, u32[]{:S(2)}) collective-permute-start(bf16[528,128]{1,0:T(8,128)(2,1)S(1)} %get-tuple-element.94), channel_id=1, source_target_pairs={{0,4},{4,0},{8,12},{12,8},{1,5},{5,1},{9,13},{13,9},{2,6},{6,2},{1... | collective-permute-start | bytes 405512 | tf_op jit(solution)/shard_map/ppermute | solution.py:287
  190.4 10.3 %collective-permute-start.38 = (bf16[8,64,128]{2,1,0:T(8,128)(2,1)S(1)}, bf16[8,64,128]{2,1,0:T(8,128)(2,1)S(1)}, u32[]{:S(2)}, u32[]{:S(2)}) collective-permute-start(bf16[8,64,128]{2,1,0:T(8,128)(2,1)S(1)} %get-tuple-element.96.refs_0_), channel_id=1, source_target_pairs={{0,8},{4,12},{8,0},{12,4},{1,9},{5,13},{9,1},{13,5},{2,10},{6,14},... | collective-permute-start | bytes 393224 | tf_op jit(solution)/shard_map/ppermute | solution.py:287
  190.4 10.3 %collective-permute-start.37 = (bf16[8,64,128]{2,1,0:T(8,128)(2,1)S(1)}, bf16[8,64,128]{2,1,0:T(8,128)(2,1)S(1)}, u32[]{:S(2)}, u32[]{:S(2)}) collective-permute-start(bf16[8,64,128]{2,1,0:T(8,128)(2,1)S(1)} %get-tuple-element.96.refs_0_), channel_id=1, source_target_pairs={{0,4},{4,0},{8,12},{12,8},{1,5},{5,1},{9,13},{13,9},{2,6},{6,2},{1... | collective-permute-start | bytes 393224 | tf_op jit(solution)/shard_map/ppermute | solution.py:287
  211.7 8.4 %collective-permute-start.42 = (bf16[528,128]{1,0:T(8,128)(2,1)S(1)}, bf16[528,128]{1,0:T(8,128)(2,1)S(1)}, u32[]{:S(2)}, u32[]{:S(2)}) collective-permute-start(bf16[528,128]{1,0:T(8,128)(2,1)S(1)} %get-tuple-element.99), channel_id=1, source_target_pairs={{0,12},{4,8},{8,4},{12,0},{1,13},{5,9},{9,5},{13,1},{2,14},{6,10},... | collective-permute-start | bytes 405512 | tf_op jit(solution)/shard_map/ppermute | solution.py:287
  213.6 11.4 %collective-permute-start.43 = (bf16[528,128]{1,0:T(8,128)(2,1)S(1)}, bf16[528,128]{1,0:T(8,128)(2,1)S(1)}, u32[]{:S(2)}, u32[]{:S(2)}) collective-permute-start(bf16[528,128]{1,0:T(8,128)(2,1)S(1)} %get-tuple-element.100), channel_id=1, source_target_pairs={{0,8},{4,12},{8,0},{12,4},{1,9},{5,13},{9,1},{13,5},{2,10},{6,14},... | collective-permute-start | bytes 405512 | tf_op jit(solution)/shard_map/ppermute | solution.py:287
  213.6 11.4 %collective-permute-start.44 = (bf16[528,128]{1,0:T(8,128)(2,1)S(1)}, bf16[528,128]{1,0:T(8,128)(2,1)S(1)}, u32[]{:S(2)}, u32[]{:S(2)}) collective-permute-start(bf16[528,128]{1,0:T(8,128)(2,1)S(1)} %get-tuple-element.101), channel_id=1, source_target_pairs={{0,4},{4,0},{8,12},{12,8},{1,5},{5,1},{9,13},{13,9},{2,6},{6,2},{1... | collective-permute-start | bytes 405512 | tf_op jit(solution)/shard_map/ppermute | solution.py:287
  227.2 10.3 %collective-permute-start.46 = (bf16[8,64,128]{2,1,0:T(8,128)(2,1)S(1)}, bf16[8,64,128]{2,1,0:T(8,128)(2,1)S(1)}, u32[]{:S(2)}, u32[]{:S(2)}) collective-permute-start(bf16[8,64,128]{2,1,0:T(8,128)(2,1)S(1)} %get-tuple-element.102.refs_0_), channel_id=1, source_target_pairs={{0,8},{4,12},{8,0},{12,4},{1,9},{5,13},{9,1},{13,5},{2,10},{6,14},... | collective-permute-start | bytes 393224 | tf_op jit(solution)/shard_map/ppermute | solution.py:287
  227.2 10.3 %collective-permute-start.45 = (bf16[8,64,128]{2,1,0:T(8,128)(2,1)S(1)}, bf16[8,64,128]{2,1,0:T(8,128)(2,1)S(1)}, u32[]{:S(2)}, u32[]{:S(2)}) collective-permute-start(bf16[8,64,128]{2,1,0:T(8,128)(2,1)S(1)} %get-tuple-element.102.refs_0_), channel_id=1, source_target_pairs={{0,4},{4,0},{8,12},{12,8},{1,5},{5,1},{9,13},{13,9},{2,6},{6,2},{1... | collective-permute-start | bytes 393224 | tf_op jit(solution)/shard_map/ppermute | solution.py:287
  240.8 8.4 %collective-permute-start.49 = (f32[8,64,128]{2,1,0:T(8,128)S(1)}, f32[8,64,128]{2,1,0:T(8,128)S(1)}, u32[]{:S(2)}, u32[]{:S(2)}) collective-permute-start(f32[8,64,128]{2,1,0:T(8,128)S(1)} %add.27.refs_0_), channel_id=1, source_target_pairs={{0,2},{1,3},{2,0},{3,1},{4,6},{5,7},{6,4},{7,5},{8,10},{9,11},{10,... | collective-permute-start | bytes 786440 | tf_op jit(solution)/shard_map/ppermute | solution.py:287
  (21 other events, 130.4 us)

commit v2 on v1

--- a/solution.py
+++ b/solution.py
@@ -69,7 +69,7 @@
     get_gid = fetch(gid_hbm, gid_ref, 3)
     get_rows = [fetch(x_hbm.at[row], xv_ref.at[row], 4 + row) for row in range(row_blocks)]
     slots = slots_ref.shape[1]
-    me = me_ref[0]
+    me = (me_ref[0] >> 1)
     samp_count = picks_ref.shape[1] // sel
     before = lax.rem(me + samp_count - 1, samp_count)
     for step in range(STEPS):
@@ -126,9 +126,14 @@
             out_ref[row, j] = x_ref[row, j].T
 
 
+def join_classes(core, own, other):
+    return jnp.concatenate([jnp.where(core == 0, own, other), jnp.where(core == 0, other, own)], axis=0)
+
+
 def forward_kernel(step, row_blocks, me_ref, slots_ref, cols_ref, xt_ref, *refs):
-    parts, (z_ref, wall) = refs[:-2], refs[-2:]
-    me = me_ref[0]
+    count = 2 if step is None else 1
+    parts, outs, wall = refs[: -1 - count], refs[-1 - count : -1], refs[-1]
+    me = (me_ref[0] >> 1)
     per_row, depth, rows = xt_ref.shape[1:]
     if len(parts) > 1:
         size = parts[0].shape[0]
@@ -139,10 +144,16 @@
         weights = wall
     else:
         weights = parts[0]
-    for slot in range(z_ref.shape[0]):
+    for slot in range(outs[0].shape[0]):
         row = slot if step is None else slots_ref[step, slot]
         tiles = jnp.concatenate([weights[cols_ref[j, me * row_blocks + row]] for j in range(per_row)], axis=1)
-        z_ref[slot] = jnp.dot(tiles, xt_ref[row].reshape(per_row * depth, rows), preferred_element_type=F32)
+        piece = jnp.dot(tiles, xt_ref[row].reshape(per_row * depth, rows), preferred_element_type=F32)
+        if step is None:
+            half = outs[0].shape[1]
+            outs[0][slot] = jnp.where((me_ref[0] & 1) == 0, piece[:half], piece[half:])
+            outs[1][slot] = jnp.where((me_ref[0] & 1) == 0, piece[half:], piece[:half])
+        else:
+            outs[0][slot] = piece
 
 
 def send_out(n_samp, me, acc, own_ref, sends, tail):
@@ -182,7 +193,7 @@
     halves, refs = refs[: 2 * chunks], refs[2 * chunks :]
     (own_ref, loss_ref), rests, refs = refs[:2], refs[2 : 1 + chunks], refs[1 + chunks :]
     sends, acc = refs[:-1], refs[-1]
-    me = me_ref[0]
+    me = (me_ref[0] >> 1)
     acc[...] = jnp.zeros_like(acc)
     classes = bounds[-1][1]
     weight = q_ref[...] / counts_ref[step]
@@ -222,7 +233,7 @@
 
 def more_grad_kernel(step, n_samp, row_blocks, me_ref, slots_ref, cols_ref, x_ref, dz_ref, own_ref, *refs):
     sends, acc = refs[:-1], refs[-1]
-    me = me_ref[0]
+    me = (me_ref[0] >> 1)
     acc[...] = jnp.zeros_like(acc)
     for slot in range(slots_ref.shape[1]):
         local = slots_ref[step, slot]
@@ -238,7 +249,7 @@
         own = own_ref[col]
         if len(recvs) == 1:
             parts = [
-                jnp.where(me_ref[0] == i, own, recvs[0][i, span, :].astype(F32)) for i in range(recvs[0].shape[0])
+                jnp.where((me_ref[0] >> 1) == i, own, recvs[0][i, span, :].astype(F32)) for i in range(recvs[0].shape[0])
             ]
         else:
             parts = [own] + [recv[span, :].astype(F32) for recv in recvs]
@@ -275,11 +286,9 @@
     new_weights(rate, me_ref, own_ref, w_ref, recvs, outs[1] if keep else None, outs[0])
 
 
-def scores_kernel(bounds, *refs):
-    out_ref = refs[-1]
-    for h, (low, high) in enumerate(bounds):
-        for block in range(refs[0].shape[0]):
-            out_ref[low:high, block * LANES : (block + 1) * LANES] = refs[2 * h][block] + refs[2 * h + 1][block]
+def scores_kernel(me_ref, mine_ref, other_ref, out_ref):
+    for block in range(mine_ref.shape[0]):
+        out_ref[:, block * LANES : (block + 1) * LANES] = join_classes((me_ref[0] & 1), mine_ref[block], other_ref[block])
 
 
 def swap(value, axis, mask):
@@ -315,7 +324,7 @@
     slots = min(row_blocks, sel - 1 + LEND)
     size = col_blocks // n_samp
     direct = 2 < n_samp <= 8
-    me = lax.axis_index("samp").astype(jnp.int32).reshape(1)
+    me = (lax.axis_index("samp") * 2 + (lax.axis_index("feat") & 1)).astype(jnp.int32).reshape(1)
     label_rows = labels.reshape(total_blocks, block_size)
     gid_rows = group_ids.reshape(total_blocks, block_size)
     cols = block_cols.T
@@ -366,12 +375,15 @@
         )(data)
 
     def forward(parts, step, width):
-        count = row_blocks if step is None else slots
+        if step is None:
+            outs = (blocks(row_blocks, width // 2, F32),) * 2
+        else:
+            outs = (blocks(slots, width, F32),)
         return pl.pallas_call(
             functools.partial(forward_kernel, step, row_blocks),
-            out_shape=blocks(count, width, F32),
+            out_shape=outs,
             in_specs=[SM, SM, SM] + [VM] * (1 + len(parts)),
-            out_specs=VM,
+            out_specs=(VM,) * len(outs),
             scratch_shapes=[pltpu.VMEM((col_blocks, width, block_size), BF16)],
             compiler_params=PARAMS,
             cost_estimate=cost(work * width, work),
@@ -456,7 +468,7 @@
         return news, logits, new_q
 
     def halves_of(parts, step):
-        return [feat_halves(forward(part, step, width)) for part, width in zip(parts, widths, strict=True)]
+        return [feat_halves(forward(part, step, width)[0]) for part, width in zip(parts, widths, strict=True)]
 
     flipped = []
     adversary = jnp.full((GRP, LANES), 1.0 / GRP, F32)
@@ -468,15 +480,19 @@
         if step + 1 < STEPS:
             states = states_new
             halves = halves_of(parts, step + 1)
-    final = halves_of(parts, None)
+    mine, give = forward(parts[0], None, classes)
+    mine, mask = mine + swap(give, "feat", 1), 2
+    while mask < n_feat:
+        mine = mine + swap(mine, "feat", mask)
+        mask *= 2
     scores = pl.pallas_call(
-        functools.partial(scores_kernel, bounds),
+        scores_kernel,
         out_shape=shape((classes, row_blocks * block_size), F32),
-        in_specs=[VM] * (2 * chunks),
+        in_specs=[SM, VM, VM],
         out_specs=VM,
         compiler_params=PARAMS,
         name="scores",
-    )(*sum(final, ()))
+    )(me, mine, swap(mine, "feat", 1))
     return (scores.T, adversary[:, 0])
 
 

time: 250 us -> 248 us (level)
    ppermute x50 -> x51, waiting for transfers between devices: 156 us -> 154 us  [swap(): return lax.ppermute(value, axis, [(i, i ^ mask) for i in range(count)])]
    ppermute x50 -> x51, starting transfers between devices: 66.9 us -> 66.8 us  [swap(): return lax.ppermute(value, axis, [(i, i ^ mask) for i in range(count)])]
  transfers between devices with their start and end apart: 50 -> 51, of which waited for: 38 -> 39; matrix products, arithmetic and copies ran while one was open for 0% -> 0% of each run, Pallas kernels for 0% -> 0%
where the time goes in v2:
time: 248 us
  waiting for transfers between devices  154 us (62%)
  starting transfers between devices  66.8 us (27%)
  Pallas kernels  25.4 us (10%)
    ppermute x51, waiting for transfers between devices, swap(): return lax.ppermute(value, axis, [(i, i ^ mask) for i in range(count)])  154 us
    ppermute x51, starting transfers between devices, swap(): return lax.ppermute(value, axis, [(i, i ^ mask) for i in range(count)])  66.8 us
    pallas_call x6, Pallas kernels, evaluate(): pl.pallas_call(functools.partial(grad_kernel, step, n_samp, row_blocks, b...  9.9 us
    pallas_call x6, Pallas kernels, forward(): pl.pallas_call(functools.partial(forward_kernel, step, row_blocks), out_s...  8.63 us
  transfers between devices with their start and end apart: 51, of which 39 were waited for; matrix products, arithmetic and copies ran while one was open for 0% of the time, Pallas kernels for 0%

profile of v2, /device:TPU:0, one launch (start us, length us, event | category | flops | bytes accessed | tf_op | source)
XLA Modules:
  0.0 248.3 jit_solution(15604137592283353841)
XLA Ops:
  0.7 4.0 %setup.1 = (s32[3,5]{1,0:T(4,128)S(1)}, s32[3,5]{1,0:T(4,128)S(1)}, f32[3,8,128]{2,1,0:T(8,128)S(1)}, bf16[8,16,128,128]{3,2,1,0:T(8,128)(2,1)S(1)}, f32[8,64,12...) custom-call(s32[1]{0:T(128)} %bitcast.me_ref, s32[3,16]{1,0:T(4,128)} %picks_hbm.1, s32[16,32]{1,0:T(8,128)} %bitcast.6, ...), custom_call_target="tpu_custom_call" | custom-call | tf_op jit(solution)/shard_map/setup/pallas_call | solution.py:340
  9.2 4.5 %collective-permute-done.1.refs_1_ = f32[5,64,128]{2,1,0:T(8,128)S(1)} collective-permute-done((f32[5,64,128]{2,1,0:T(8,128)S(1)}, f32[5,64,128]{2,1,0:T(8,128)S(1)}, u32[]{:S(2)}, u32[]{:S(2)}) %collective-permute-start.1) | collective-permute-done | bytes 163872 | tf_op jit(solution)/shard_map/ppermute | solution.py:296
  15.4 3.9 %collective-permute-start.2 = (f32[520,128]{1,0:T(8,128)S(1)}, f32[520,128]{1,0:T(8,128)S(1)}, u32[]{:S(2)}, u32[]{:S(2)}) collective-permute-start(f32[520,128]{1,0:T(8,128)S(1)} %get-tuple-element.64), channel_id=1, source_target_pairs={{0,12},{4,8},{8,4},{12,0},{1,13},{5,9},{9,5},{13,1},{2,14},{6,10},... | collective-permute-start | bytes 798728 | tf_op jit(solution)/shard_map/ppermute | solution.py:296
  19.9 6.8 %collective-permute-done.2.refs_0_ = f32[520,128]{1,0:T(8,128)S(1)} collective-permute-done((f32[520,128]{1,0:T(8,128)S(1)}, f32[520,128]{1,0:T(8,128)S(1)}, u32[]{:S(2)}, u32[]{:S(2)}) %collective-permute-start.2) | collective-permute-done | bytes 266272 | tf_op jit(solution)/shard_map/ppermute | solution.py:296
  26.7 14.7 %collective-permute-done.3.refs_1_ = f32[520,128]{1,0:T(8,128)S(1)} collective-permute-done((f32[520,128]{1,0:T(8,128)S(1)}, f32[520,128]{1,0:T(8,128)S(1)}, u32[]{:S(2)}, u32[]{:S(2)}) %collective-permute-start.3) | collective-permute-done | bytes 266272 | tf_op jit(solution)/shard_map/ppermute | solution.py:296
  49.8 4.4 %collective-permute-done.6.refs_2_ = bf16[8,64,128]{2,1,0:T(8,128)(2,1)S(1)} collective-permute-done((bf16[8,64,128]{2,1,0:T(8,128)(2,1)S(1)}, bf16[8,64,128]{2,1,0:T(8,128)(2,1)S(1)}, u32[]{:S(2)}, u32[]{:S(2)}) %collective-permute-start.6) | collective-permute-done | bytes 131104 | tf_op jit(solution)/shard_map/ppermute | solution.py:296
  58.6 4.8 %collective-permute-done.9.refs_1_ = f32[5,64,128]{2,1,0:T(8,128)S(1)} collective-permute-done((f32[5,64,128]{2,1,0:T(8,128)S(1)}, f32[5,64,128]{2,1,0:T(8,128)S(1)}, u32[]{:S(2)}, u32[]{:S(2)}) %collective-permute-start.9) | collective-permute-done | bytes 163872 | tf_op jit(solution)/shard_map/ppermute | solution.py:296
  69.5 4.0 %collective-permute-done.10.refs_0_ = bf16[528,128]{1,0:T(8,128)(2,1)S(1)} collective-permute-done((bf16[528,128]{1,0:T(8,128)(2,1)S(1)}, bf16[528,128]{1,0:T(8,128)(2,1)S(1)}, u32[]{:S(2)}, u32[]{:S(2)}) %collective-permute-start.10) | collective-permute-done | bytes 135200 | tf_op jit(solution)/shard_map/ppermute | solution.py:296
  73.4 4.1 %collective-permute-done.11.refs_1_ = bf16[528,128]{1,0:T(8,128)(2,1)S(1)} collective-permute-done((bf16[528,128]{1,0:T(8,128)(2,1)S(1)}, bf16[528,128]{1,0:T(8,128)(2,1)S(1)}, u32[]{:S(2)}, u32[]{:S(2)}) %collective-permute-start.11) | collective-permute-done | bytes 135200 | tf_op jit(solution)/shard_map/ppermute | solution.py:296
  82.2 3.9 %collective-permute-done.15.refs_3_ = bf16[8,64,128]{2,1,0:T(8,128)(2,1)S(1)} collective-permute-done((bf16[8,64,128]{2,1,0:T(8,128)(2,1)S(1)}, bf16[8,64,128]{2,1,0:T(8,128)(2,1)S(1)}, u32[]{:S(2)}, u32[]{:S(2)}) %collective-permute-start.15) | collective-permute-done | bytes 131104 | tf_op jit(solution)/shard_map/ppermute | solution.py:296
  86.1 4.7 %collective-permute-done.14.refs_2_ = bf16[8,64,128]{2,1,0:T(8,128)(2,1)S(1)} collective-permute-done((bf16[8,64,128]{2,1,0:T(8,128)(2,1)S(1)}, bf16[8,64,128]{2,1,0:T(8,128)(2,1)S(1)}, u32[]{:S(2)}, u32[]{:S(2)}) %collective-permute-start.14) | collective-permute-done | bytes 131104 | tf_op jit(solution)/shard_map/ppermute | solution.py:296
  95.2 4.8 %collective-permute-done.17.refs_1_ = f32[5,64,128]{2,1,0:T(8,128)S(1)} collective-permute-done((f32[5,64,128]{2,1,0:T(8,128)S(1)}, f32[5,64,128]{2,1,0:T(8,128)S(1)}, u32[]{:S(2)}, u32[]{:S(2)}) %collective-permute-start.17) | collective-permute-done | bytes 163872 | tf_op jit(solution)/shard_map/ppermute | solution.py:296
  106.0 3.9 %collective-permute-done.18.refs_0_ = bf16[528,128]{1,0:T(8,128)(2,1)S(1)} collective-permute-done((bf16[528,128]{1,0:T(8,128)(2,1)S(1)}, bf16[528,128]{1,0:T(8,128)(2,1)S(1)}, u32[]{:S(2)}, u32[]{:S(2)}) %collective-permute-start.18) | collective-permute-done | bytes 135200 | tf_op jit(solution)/shard_map/ppermute | solution.py:296
  110.0 4.4 %collective-permute-done.19.refs_1_ = bf16[528,128]{1,0:T(8,128)(2,1)S(1)} collective-permute-done((bf16[528,128]{1,0:T(8,128)(2,1)S(1)}, bf16[528,128]{1,0:T(8,128)(2,1)S(1)}, u32[]{:S(2)}, u32[]{:S(2)}) %collective-permute-start.19) | collective-permute-done | bytes 135200 | tf_op jit(solution)/shard_map/ppermute | solution.py:296
  119.0 3.9 %collective-permute-done.23.refs_3_ = bf16[8,64,128]{2,1,0:T(8,128)(2,1)S(1)} collective-permute-done((bf16[8,64,128]{2,1,0:T(8,128)(2,1)S(1)}, bf16[8,64,128]{2,1,0:T(8,128)(2,1)S(1)}, u32[]{:S(2)}, u32[]{:S(2)}) %collective-permute-start.23) | collective-permute-done | bytes 131104 | tf_op jit(solution)/shard_map/ppermute | solution.py:296
  122.9 4.5 %collective-permute-done.22.refs_2_ = bf16[8,64,128]{2,1,0:T(8,128)(2,1)S(1)} collective-permute-done((bf16[8,64,128]{2,1,0:T(8,128)(2,1)S(1)}, bf16[8,64,128]{2,1,0:T(8,128)(2,1)S(1)}, u32[]{:S(2)}, u32[]{:S(2)}) %collective-permute-start.22) | collective-permute-done | bytes 131104 | tf_op jit(solution)/shard_map/ppermute | solution.py:296
  131.8 4.8 %collective-permute-done.25.refs_1_ = f32[5,64,128]{2,1,0:T(8,128)S(1)} collective-permute-done((f32[5,64,128]{2,1,0:T(8,128)S(1)}, f32[5,64,128]{2,1,0:T(8,128)S(1)}, u32[]{:S(2)}, u32[]{:S(2)}) %collective-permute-start.25) | collective-permute-done | bytes 163872 | tf_op jit(solution)/shard_map/ppermute | solution.py:296
  142.7 3.9 %collective-permute-done.26.refs_0_ = bf16[528,128]{1,0:T(8,128)(2,1)S(1)} collective-permute-done((bf16[528,128]{1,0:T(8,128)(2,1)S(1)}, bf16[528,128]{1,0:T(8,128)(2,1)S(1)}, u32[]{:S(2)}, u32[]{:S(2)}) %collective-permute-start.26) | collective-permute-done | bytes 135200 | tf_op jit(solution)/shard_map/ppermute | solution.py:296
  146.6 4.9 %collective-permute-done.27.refs_1_ = bf16[528,128]{1,0:T(8,128)(2,1)S(1)} collective-permute-done((bf16[528,128]{1,0:T(8,128)(2,1)S(1)}, bf16[528,128]{1,0:T(8,128)(2,1)S(1)}, u32[]{:S(2)}, u32[]{:S(2)}) %collective-permute-start.27) | collective-permute-done | bytes 135200 | tf_op jit(solution)/shard_map/ppermute | solution.py:296
  156.1 3.9 %collective-permute-done.31.refs_3_ = bf16[8,64,128]{2,1,0:T(8,128)(2,1)S(1)} collective-permute-done((bf16[8,64,128]{2,1,0:T(8,128)(2,1)S(1)}, bf16[8,64,128]{2,1,0:T(8,128)(2,1)S(1)}, u32[]{:S(2)}, u32[]{:S(2)}) %collective-permute-start.31) | collective-permute-done | bytes 131104 | tf_op jit(solution)/shard_map/ppermute | solution.py:296
  160.0 4.0 %collective-permute-done.30.refs_2_ = bf16[8,64,128]{2,1,0:T(8,128)(2,1)S(1)} collective-permute-done((bf16[8,64,128]{2,1,0:T(8,128)(2,1)S(1)}, bf16[8,64,128]{2,1,0:T(8,128)(2,1)S(1)}, u32[]{:S(2)}, u32[]{:S(2)}) %collective-permute-start.30) | collective-permute-done | bytes 131104 | tf_op jit(solution)/shard_map/ppermute | solution.py:296
  168.4 4.8 %collective-permute-done.33.refs_1_ = f32[5,64,128]{2,1,0:T(8,128)S(1)} collective-permute-done((f32[5,64,128]{2,1,0:T(8,128)S(1)}, f32[5,64,128]{2,1,0:T(8,128)S(1)}, u32[]{:S(2)}, u32[]{:S(2)}) %collective-permute-start.33) | collective-permute-done | bytes 163872 | tf_op jit(solution)/shard_map/ppermute | solution.py:296
  179.3 3.9 %collective-permute-done.34.refs_0_ = bf16[528,128]{1,0:T(8,128)(2,1)S(1)} collective-permute-done((bf16[528,128]{1,0:T(8,128)(2,1)S(1)}, bf16[528,128]{1,0:T(8,128)(2,1)S(1)}, u32[]{:S(2)}, u32[]{:S(2)}) %collective-permute-start.34) | collective-permute-done | bytes 135200 | tf_op jit(solution)/shard_map/ppermute | solution.py:296
  183.2 4.9 %collective-permute-done.35.refs_1_ = bf16[528,128]{1,0:T(8,128)(2,1)S(1)} collective-permute-done((bf16[528,128]{1,0:T(8,128)(2,1)S(1)}, bf16[528,128]{1,0:T(8,128)(2,1)S(1)}, u32[]{:S(2)}, u32[]{:S(2)}) %collective-permute-start.35) | collective-permute-done | bytes 135200 | tf_op jit(solution)/shard_map/ppermute | solution.py:296
  192.7 3.9 %collective-permute-done.39.refs_3_ = bf16[8,64,128]{2,1,0:T(8,128)(2,1)S(1)} collective-permute-done((bf16[8,64,128]{2,1,0:T(8,128)(2,1)S(1)}, bf16[8,64,128]{2,1,0:T(8,128)(2,1)S(1)}, u32[]{:S(2)}, u32[]{:S(2)}) %collective-permute-start.39) | collective-permute-done | bytes 131104 | tf_op jit(solution)/shard_map/ppermute | solution.py:296
  196.6 4.0 %collective-permute-done.38.refs_2_ = bf16[8,64,128]{2,1,0:T(8,128)(2,1)S(1)} collective-permute-done((bf16[8,64,128]{2,1,0:T(8,128)(2,1)S(1)}, bf16[8,64,128]{2,1,0:T(8,128)(2,1)S(1)}, u32[]{:S(2)}, u32[]{:S(2)}) %collective-permute-start.38) | collective-permute-done | bytes 131104 | tf_op jit(solution)/shard_map/ppermute | solution.py:296
  205.2 4.8 %collective-permute-done.41.refs_1_ = f32[5,64,128]{2,1,0:T(8,128)S(1)} collective-permute-done((f32[5,64,128]{2,1,0:T(8,128)S(1)}, f32[5,64,128]{2,1,0:T(8,128)S(1)}, u32[]{:S(2)}, u32[]{:S(2)}) %collective-permute-start.41) | collective-permute-done | bytes 163872 | tf_op jit(solution)/shard_map/ppermute | solution.py:296
  216.1 3.9 %collective-permute-done.42.refs_0_ = bf16[528,128]{1,0:T(8,128)(2,1)S(1)} collective-permute-done((bf16[528,128]{1,0:T(8,128)(2,1)S(1)}, bf16[528,128]{1,0:T(8,128)(2,1)S(1)}, u32[]{:S(2)}, u32[]{:S(2)}) %collective-permute-start.42) | collective-permute-done | bytes 135200 | tf_op jit(solution)/shard_map/ppermute | solution.py:296
  220.0 4.9 %collective-permute-done.43.refs_1_ = bf16[528,128]{1,0:T(8,128)(2,1)S(1)} collective-permute-done((bf16[528,128]{1,0:T(8,128)(2,1)S(1)}, bf16[528,128]{1,0:T(8,128)(2,1)S(1)}, u32[]{:S(2)}, u32[]{:S(2)}) %collective-permute-start.43) | collective-permute-done | bytes 135200 | tf_op jit(solution)/shard_map/ppermute | solution.py:296
  229.5 3.9 %collective-permute-done.47.refs_3_ = bf16[8,64,128]{2,1,0:T(8,128)(2,1)S(1)} collective-permute-done((bf16[8,64,128]{2,1,0:T(8,128)(2,1)S(1)}, bf16[8,64,128]{2,1,0:T(8,128)(2,1)S(1)}, u32[]{:S(2)}, u32[]{:S(2)}) %collective-permute-start.47) | collective-permute-done | bytes 131104 | tf_op jit(solution)/shard_map/ppermute | solution.py:296
  233.4 3.9 %collective-permute-done.46.refs_2_ = bf16[8,64,128]{2,1,0:T(8,128)(2,1)S(1)} collective-permute-done((bf16[8,64,128]{2,1,0:T(8,128)(2,1)S(1)}, bf16[8,64,128]{2,1,0:T(8,128)(2,1)S(1)}, u32[]{:S(2)}, u32[]{:S(2)}) %collective-permute-start.46) | collective-permute-done | bytes 131104 | tf_op jit(solution)/shard_map/ppermute | solution.py:296
  242.1 4.1 %collective-permute-done.49 = f32[8,32,128]{2,1,0:T(8,128)S(1)} collective-permute-done((f32[8,32,128]{2,1,0:T(8,128)S(1)}, f32[8,32,128]{2,1,0:T(8,128)S(1)}, u32[]{:S(2)}, u32[]{:S(2)}) %collective-permute-start.49) | collective-permute-done | bytes 131104 | tf_op jit(solution)/shard_map/ppermute | solution.py:296
  (107 shorter events, 97.8 us)
Async XLA Ops:
  15.4 11.3 %collective-permute-start.2 = (f32[520,128]{1,0:T(8,128)S(1)}, f32[520,128]{1,0:T(8,128)S(1)}, u32[]{:S(2)}, u32[]{:S(2)}) collective-permute-start(f32[520,128]{1,0:T(8,128)S(1)} %get-tuple-element.64), channel_id=1, source_target_pairs={{0,12},{4,8},{8,4},{12,0},{1,13},{5,9},{9,5},{13,1},{2,14},{6,10},... | collective-permute-start | bytes 798728 | tf_op jit(solution)/shard_map/ppermute | solution.py:296
  19.3 22.1 %collective-permute-start.3 = (f32[520,128]{1,0:T(8,128)S(1)}, f32[520,128]{1,0:T(8,128)S(1)}, u32[]{:S(2)}, u32[]{:S(2)}) collective-permute-start(f32[520,128]{1,0:T(8,128)S(1)} %get-tuple-element.65), channel_id=1, source_target_pairs={{0,8},{4,12},{8,0},{12,4},{1,9},{5,13},{9,1},{13,5},{2,10},{6,14},... | collective-permute-start | bytes 798728 | tf_op jit(solution)/shard_map/ppermute | solution.py:296
  19.3 22.1 %collective-permute-start.4 = (f32[520,128]{1,0:T(8,128)S(1)}, f32[520,128]{1,0:T(8,128)S(1)}, u32[]{:S(2)}, u32[]{:S(2)}) collective-permute-start(f32[520,128]{1,0:T(8,128)S(1)} %get-tuple-element.66), channel_id=1, source_target_pairs={{0,4},{4,0},{8,12},{12,8},{1,5},{5,1},{9,13},{13,9},{2,6},{6,2},{1... | collective-permute-start | bytes 798728 | tf_op jit(solution)/shard_map/ppermute | solution.py:296
  44.2 10.0 %collective-permute-start.6 = (bf16[8,64,128]{2,1,0:T(8,128)(2,1)S(1)}, bf16[8,64,128]{2,1,0:T(8,128)(2,1)S(1)}, u32[]{:S(2)}, u32[]{:S(2)}) collective-permute-start(bf16[8,64,128]{2,1,0:T(8,128)(2,1)S(1)} %get-tuple-element.68.refs_0_), channel_id=1, source_target_pairs={{0,8},{4,12},{8,0},{12,4},{1,9},{5,13},{9,1},{13,5},{2,10},{6,14},... | collective-permute-start | bytes 393224 | tf_op jit(solution)/shard_map/ppermute | solution.py:296
  44.2 10.0 %collective-permute-start.5 = (bf16[8,64,128]{2,1,0:T(8,128)(2,1)S(1)}, bf16[8,64,128]{2,1,0:T(8,128)(2,1)S(1)}, u32[]{:S(2)}, u32[]{:S(2)}) collective-permute-start(bf16[8,64,128]{2,1,0:T(8,128)(2,1)S(1)} %get-tuple-element.68.refs_0_), channel_id=1, source_target_pairs={{0,4},{4,0},{8,12},{12,8},{1,5},{5,1},{9,13},{13,9},{2,6},{6,2},{1... | collective-permute-start | bytes 393224 | tf_op jit(solution)/shard_map/ppermute | solution.py:296
  65.0 8.4 %collective-permute-start.10 = (bf16[528,128]{1,0:T(8,128)(2,1)S(1)}, bf16[528,128]{1,0:T(8,128)(2,1)S(1)}, u32[]{:S(2)}, u32[]{:S(2)}) collective-permute-start(bf16[528,128]{1,0:T(8,128)(2,1)S(1)} %get-tuple-element.71), channel_id=1, source_target_pairs={{0,12},{4,8},{8,4},{12,0},{1,13},{5,9},{9,5},{13,1},{2,14},{6,10},... | collective-permute-start | bytes 405512 | tf_op jit(solution)/shard_map/ppermute | solution.py:296
  66.4 11.2 %collective-permute-start.11 = (bf16[528,128]{1,0:T(8,128)(2,1)S(1)}, bf16[528,128]{1,0:T(8,128)(2,1)S(1)}, u32[]{:S(2)}, u32[]{:S(2)}) collective-permute-start(bf16[528,128]{1,0:T(8,128)(2,1)S(1)} %get-tuple-element.72), channel_id=1, source_target_pairs={{0,8},{4,12},{8,0},{12,4},{1,9},{5,13},{9,1},{13,5},{2,10},{6,14},... | collective-permute-start | bytes 405512 | tf_op jit(solution)/shard_map/ppermute | solution.py:296
  66.4 11.2 %collective-permute-start.12 = (bf16[528,128]{1,0:T(8,128)(2,1)S(1)}, bf16[528,128]{1,0:T(8,128)(2,1)S(1)}, u32[]{:S(2)}, u32[]{:S(2)}) collective-permute-start(bf16[528,128]{1,0:T(8,128)(2,1)S(1)} %get-tuple-element.73), channel_id=1, source_target_pairs={{0,4},{4,0},{8,12},{12,8},{1,5},{5,1},{9,13},{13,9},{2,6},{6,2},{1... | collective-permute-start | bytes 405512 | tf_op jit(solution)/shard_map/ppermute | solution.py:296
  79.9 10.9 %collective-permute-start.14 = (bf16[8,64,128]{2,1,0:T(8,128)(2,1)S(1)}, bf16[8,64,128]{2,1,0:T(8,128)(2,1)S(1)}, u32[]{:S(2)}, u32[]{:S(2)}) collective-permute-start(bf16[8,64,128]{2,1,0:T(8,128)(2,1)S(1)} %get-tuple-element.75.refs_0_), channel_id=1, source_target_pairs={{0,8},{4,12},{8,0},{12,4},{1,9},{5,13},{9,1},{13,5},{2,10},{6,14},... | collective-permute-start | bytes 393224 | tf_op jit(solution)/shard_map/ppermute | solution.py:296
  79.9 10.9 %collective-permute-start.13 = (bf16[8,64,128]{2,1,0:T(8,128)(2,1)S(1)}, bf16[8,64,128]{2,1,0:T(8,128)(2,1)S(1)}, u32[]{:S(2)}, u32[]{:S(2)}) collective-permute-start(bf16[8,64,128]{2,1,0:T(8,128)(2,1)S(1)} %get-tuple-element.75.refs_0_), channel_id=1, source_target_pairs={{0,4},{4,0},{8,12},{12,8},{1,5},{5,1},{9,13},{13,9},{2,6},{6,2},{1... | collective-permute-start | bytes 393224 | tf_op jit(solution)/shard_map/ppermute | solution.py:296
  101.6 8.4 %collective-permute-start.18 = (bf16[528,128]{1,0:T(8,128)(2,1)S(1)}, bf16[528,128]{1,0:T(8,128)(2,1)S(1)}, u32[]{:S(2)}, u32[]{:S(2)}) collective-permute-start(bf16[528,128]{1,0:T(8,128)(2,1)S(1)} %get-tuple-element.79), channel_id=1, source_target_pairs={{0,12},{4,8},{8,4},{12,0},{1,13},{5,9},{9,5},{13,1},{2,14},{6,10},... | collective-permute-start | bytes 405512 | tf_op jit(solution)/shard_map/ppermute | solution.py:296
  103.5 10.8 %collective-permute-start.19 = (bf16[528,128]{1,0:T(8,128)(2,1)S(1)}, bf16[528,128]{1,0:T(8,128)(2,1)S(1)}, u32[]{:S(2)}, u32[]{:S(2)}) collective-permute-start(bf16[528,128]{1,0:T(8,128)(2,1)S(1)} %get-tuple-element.80), channel_id=1, source_target_pairs={{0,8},{4,12},{8,0},{12,4},{1,9},{5,13},{9,1},{13,5},{2,10},{6,14},... | collective-permute-start | bytes 405512 | tf_op jit(solution)/shard_map/ppermute | solution.py:296
  103.5 10.8 %collective-permute-start.20 = (bf16[528,128]{1,0:T(8,128)(2,1)S(1)}, bf16[528,128]{1,0:T(8,128)(2,1)S(1)}, u32[]{:S(2)}, u32[]{:S(2)}) collective-permute-start(bf16[528,128]{1,0:T(8,128)(2,1)S(1)} %get-tuple-element.81), channel_id=1, source_target_pairs={{0,4},{4,0},{8,12},{12,8},{1,5},{5,1},{9,13},{13,9},{2,6},{6,2},{1... | collective-permute-start | bytes 405512 | tf_op jit(solution)/shard_map/ppermute | solution.py:296
  117.1 10.3 %collective-permute-start.22 = (bf16[8,64,128]{2,1,0:T(8,128)(2,1)S(1)}, bf16[8,64,128]{2,1,0:T(8,128)(2,1)S(1)}, u32[]{:S(2)}, u32[]{:S(2)}) collective-permute-start(bf16[8,64,128]{2,1,0:T(8,128)(2,1)S(1)} %get-tuple-element.83.refs_0_), channel_id=1, source_target_pairs={{0,8},{4,12},{8,0},{12,4},{1,9},{5,13},{9,1},{13,5},{2,10},{6,14},... | collective-permute-start | bytes 393224 | tf_op jit(solution)/shard_map/ppermute | solution.py:296
  117.1 10.3 %collective-permute-start.21 = (bf16[8,64,128]{2,1,0:T(8,128)(2,1)S(1)}, bf16[8,64,128]{2,1,0:T(8,128)(2,1)S(1)}, u32[]{:S(2)}, u32[]{:S(2)}) collective-permute-start(bf16[8,64,128]{2,1,0:T(8,128)(2,1)S(1)} %get-tuple-element.83.refs_0_), channel_id=1, source_target_pairs={{0,4},{4,0},{8,12},{12,8},{1,5},{5,1},{9,13},{13,9},{2,6},{6,2},{1... | collective-permute-start | bytes 393224 | tf_op jit(solution)/shard_map/ppermute | solution.py:296
  138.2 8.4 %collective-permute-start.26 = (bf16[528,128]{1,0:T(8,128)(2,1)S(1)}, bf16[528,128]{1,0:T(8,128)(2,1)S(1)}, u32[]{:S(2)}, u32[]{:S(2)}) collective-permute-start(bf16[528,128]{1,0:T(8,128)(2,1)S(1)} %get-tuple-element.86), channel_id=1, source_target_pairs={{0,12},{4,8},{8,4},{12,0},{1,13},{5,9},{9,5},{13,1},{2,14},{6,10},... | collective-permute-start | bytes 405512 | tf_op jit(solution)/shard_map/ppermute | solution.py:296
  140.1 11.4 %collective-permute-start.27 = (bf16[528,128]{1,0:T(8,128)(2,1)S(1)}, bf16[528,128]{1,0:T(8,128)(2,1)S(1)}, u32[]{:S(2)}, u32[]{:S(2)}) collective-permute-start(bf16[528,128]{1,0:T(8,128)(2,1)S(1)} %get-tuple-element.87), channel_id=1, source_target_pairs={{0,8},{4,12},{8,0},{12,4},{1,9},{5,13},{9,1},{13,5},{2,10},{6,14},... | collective-permute-start | bytes 405512 | tf_op jit(solution)/shard_map/ppermute | solution.py:296
  140.1 11.4 %collective-permute-start.28 = (bf16[528,128]{1,0:T(8,128)(2,1)S(1)}, bf16[528,128]{1,0:T(8,128)(2,1)S(1)}, u32[]{:S(2)}, u32[]{:S(2)}) collective-permute-start(bf16[528,128]{1,0:T(8,128)(2,1)S(1)} %get-tuple-element.88), channel_id=1, source_target_pairs={{0,4},{4,0},{8,12},{12,8},{1,5},{5,1},{9,13},{13,9},{2,6},{6,2},{1... | collective-permute-start | bytes 405512 | tf_op jit(solution)/shard_map/ppermute | solution.py:296
  151.7 8.4 %collective-permute-start.31 = (bf16[8,64,128]{2,1,0:T(8,128)(2,1)S(1)}, bf16[8,64,128]{2,1,0:T(8,128)(2,1)S(1)}, u32[]{:S(2)}, u32[]{:S(2)}) collective-permute-start(bf16[8,64,128]{2,1,0:T(8,128)(2,1)S(1)} %get-tuple-element.90.refs_0_), channel_id=1, source_target_pairs={{0,12},{4,8},{8,4},{12,0},{1,13},{5,9},{9,5},{13,1},{2,14},{6,10},... | collective-permute-start | bytes 393224 | tf_op jit(solution)/shard_map/ppermute | solution.py:296
  153.7 10.3 %collective-permute-start.30 = (bf16[8,64,128]{2,1,0:T(8,128)(2,1)S(1)}, bf16[8,64,128]{2,1,0:T(8,128)(2,1)S(1)}, u32[]{:S(2)}, u32[]{:S(2)}) collective-permute-start(bf16[8,64,128]{2,1,0:T(8,128)(2,1)S(1)} %get-tuple-element.90.refs_0_), channel_id=1, source_target_pairs={{0,8},{4,12},{8,0},{12,4},{1,9},{5,13},{9,1},{13,5},{2,10},{6,14},... | collective-permute-start | bytes 393224 | tf_op jit(solution)/shard_map/ppermute | solution.py:296
  153.7 10.3 %collective-permute-start.29 = (bf16[8,64,128]{2,1,0:T(8,128)(2,1)S(1)}, bf16[8,64,128]{2,1,0:T(8,128)(2,1)S(1)}, u32[]{:S(2)}, u32[]{:S(2)}) collective-permute-start(bf16[8,64,128]{2,1,0:T(8,128)(2,1)S(1)} %get-tuple-element.90.refs_0_), channel_id=1, source_target_pairs={{0,4},{4,0},{8,12},{12,8},{1,5},{5,1},{9,13},{13,9},{2,6},{6,2},{1... | collective-permute-start | bytes 393224 | tf_op jit(solution)/shard_map/ppermute | solution.py:296
  174.8 8.4 %collective-permute-start.34 = (bf16[528,128]{1,0:T(8,128)(2,1)S(1)}, bf16[528,128]{1,0:T(8,128)(2,1)S(1)}, u32[]{:S(2)}, u32[]{:S(2)}) collective-permute-start(bf16[528,128]{1,0:T(8,128)(2,1)S(1)} %get-tuple-element.94), channel_id=1, source_target_pairs={{0,12},{4,8},{8,4},{12,0},{1,13},{5,9},{9,5},{13,1},{2,14},{6,10},... | collective-permute-start | bytes 405512 | tf_op jit(solution)/shard_map/ppermute | solution.py:296
  176.7 11.4 %collective-permute-start.35 = (bf16[528,128]{1,0:T(8,128)(2,1)S(1)}, bf16[528,128]{1,0:T(8,128)(2,1)S(1)}, u32[]{:S(2)}, u32[]{:S(2)}) collective-permute-start(bf16[528,128]{1,0:T(8,128)(2,1)S(1)} %get-tuple-element.95), channel_id=1, source_target_pairs={{0,8},{4,12},{8,0},{12,4},{1,9},{5,13},{9,1},{13,5},{2,10},{6,14},... | collective-permute-start | bytes 405512 | tf_op jit(solution)/shard_map/ppermute | solution.py:296
  176.7 11.4 %collective-permute-start.36 = (bf16[528,128]{1,0:T(8,128)(2,1)S(1)}, bf16[528,128]{1,0:T(8,128)(2,1)S(1)}, u32[]{:S(2)}, u32[]{:S(2)}) collective-permute-start(bf16[528,128]{1,0:T(8,128)(2,1)S(1)} %get-tuple-element.96), channel_id=1, source_target_pairs={{0,4},{4,0},{8,12},{12,8},{1,5},{5,1},{9,13},{13,9},{2,6},{6,2},{1... | collective-permute-start | bytes 405512 | tf_op jit(solution)/shard_map/ppermute | solution.py:296
  188.3 8.4 %collective-permute-start.39 = (bf16[8,64,128]{2,1,0:T(8,128)(2,1)S(1)}, bf16[8,64,128]{2,1,0:T(8,128)(2,1)S(1)}, u32[]{:S(2)}, u32[]{:S(2)}) collective-permute-start(bf16[8,64,128]{2,1,0:T(8,128)(2,1)S(1)} %get-tuple-element.98.refs_0_), channel_id=1, source_target_pairs={{0,12},{4,8},{8,4},{12,0},{1,13},{5,9},{9,5},{13,1},{2,14},{6,10},... | collective-permute-start | bytes 393224 | tf_op jit(solution)/shard_map/ppermute | solution.py:296
  190.3 10.3 %collective-permute-start.38 = (bf16[8,64,128]{2,1,0:T(8,128)(2,1)S(1)}, bf16[8,64,128]{2,1,0:T(8,128)(2,1)S(1)}, u32[]{:S(2)}, u32[]{:S(2)}) collective-permute-start(bf16[8,64,128]{2,1,0:T(8,128)(2,1)S(1)} %get-tuple-element.98.refs_0_), channel_id=1, source_target_pairs={{0,8},{4,12},{8,0},{12,4},{1,9},{5,13},{9,1},{13,5},{2,10},{6,14},... | collective-permute-start | bytes 393224 | tf_op jit(solution)/shard_map/ppermute | solution.py:296
  190.3 10.3 %collective-permute-start.37 = (bf16[8,64,128]{2,1,0:T(8,128)(2,1)S(1)}, bf16[8,64,128]{2,1,0:T(8,128)(2,1)S(1)}, u32[]{:S(2)}, u32[]{:S(2)}) collective-permute-start(bf16[8,64,128]{2,1,0:T(8,128)(2,1)S(1)} %get-tuple-element.98.refs_0_), channel_id=1, source_target_pairs={{0,4},{4,0},{8,12},{12,8},{1,5},{5,1},{9,13},{13,9},{2,6},{6,2},{1... | collective-permute-start | bytes 393224 | tf_op jit(solution)/shard_map/ppermute | solution.py:296
  211.6 8.4 %collective-permute-start.42 = (bf16[528,128]{1,0:T(8,128)(2,1)S(1)}, bf16[528,128]{1,0:T(8,128)(2,1)S(1)}, u32[]{:S(2)}, u32[]{:S(2)}) collective-permute-start(bf16[528,128]{1,0:T(8,128)(2,1)S(1)} %get-tuple-element.101), channel_id=1, source_target_pairs={{0,12},{4,8},{8,4},{12,0},{1,13},{5,9},{9,5},{13,1},{2,14},{6,10},... | collective-permute-start | bytes 405512 | tf_op jit(solution)/shard_map/ppermute | solution.py:296
  213.5 11.4 %collective-permute-start.43 = (bf16[528,128]{1,0:T(8,128)(2,1)S(1)}, bf16[528,128]{1,0:T(8,128)(2,1)S(1)}, u32[]{:S(2)}, u32[]{:S(2)}) collective-permute-start(bf16[528,128]{1,0:T(8,128)(2,1)S(1)} %get-tuple-element.102), channel_id=1, source_target_pairs={{0,8},{4,12},{8,0},{12,4},{1,9},{5,13},{9,1},{13,5},{2,10},{6,14},... | collective-permute-start | bytes 405512 | tf_op jit(solution)/shard_map/ppermute | solution.py:296
  213.5 11.4 %collective-permute-start.44 = (bf16[528,128]{1,0:T(8,128)(2,1)S(1)}, bf16[528,128]{1,0:T(8,128)(2,1)S(1)}, u32[]{:S(2)}, u32[]{:S(2)}) collective-permute-start(bf16[528,128]{1,0:T(8,128)(2,1)S(1)} %get-tuple-element.103), channel_id=1, source_target_pairs={{0,4},{4,0},{8,12},{12,8},{1,5},{5,1},{9,13},{13,9},{2,6},{6,2},{1... | collective-permute-start | bytes 405512 | tf_op jit(solution)/shard_map/ppermute | solution.py:296
  227.1 10.3 %collective-permute-start.46 = (bf16[8,64,128]{2,1,0:T(8,128)(2,1)S(1)}, bf16[8,64,128]{2,1,0:T(8,128)(2,1)S(1)}, u32[]{:S(2)}, u32[]{:S(2)}) collective-permute-start(bf16[8,64,128]{2,1,0:T(8,128)(2,1)S(1)} %get-tuple-element.104.refs_0_), channel_id=1, source_target_pairs={{0,8},{4,12},{8,0},{12,4},{1,9},{5,13},{9,1},{13,5},{2,10},{6,14},... | collective-permute-start | bytes 393224 | tf_op jit(solution)/shard_map/ppermute | solution.py:296
  227.1 10.3 %collective-permute-start.45 = (bf16[8,64,128]{2,1,0:T(8,128)(2,1)S(1)}, bf16[8,64,128]{2,1,0:T(8,128)(2,1)S(1)}, u32[]{:S(2)}, u32[]{:S(2)}) collective-permute-start(bf16[8,64,128]{2,1,0:T(8,128)(2,1)S(1)} %get-tuple-element.104.refs_0_), channel_id=1, source_target_pairs={{0,4},{4,0},{8,12},{12,8},{1,5},{5,1},{9,13},{13,9},{2,6},{6,2},{1... | collective-permute-start | bytes 393224 | tf_op jit(solution)/shard_map/ppermute | solution.py:296
  (22 other events, 128.9 us)

commit v3 on v2

--- a/solution.py
+++ b/solution.py
@@ -56,7 +56,7 @@
 ):
     chunks = len(bounds)
     owns, zs = refs[:chunks], refs[chunks : 2 * chunks]
-    wall, picks_ref, cols_ref, gid_ref, w_ref, sems = refs[2 * chunks :]
+    wall, picks_ref, cols_ref, slot_of, gid_ref, w_ref, sems = refs[2 * chunks :]
 
     def fetch(source, target, place):
         copy = pltpu.make_async_copy(source, target, sems.at[place])
@@ -76,6 +76,10 @@
         for slot in range(slots):
             slots_ref[step, slot] = 0
             live_ref[step, slot] = 0
+    for row in range(row_blocks):
+        slot_of[row] = -1
+    for z in zs:
+        z[...] = jnp.zeros_like(z)
     get_picks.wait()
     for step in range(STEPS):
         found = jnp.int32(0)
@@ -89,6 +93,8 @@
                 def _(step=step, place=place, block=block):
                     slots_ref[step, place] = block - me * row_blocks
                     live_ref[step, place] = 1
+                    if step == 0:
+                        slot_of[block - me * row_blocks] = place
 
                 found = found + mine.astype(jnp.int32)
     get_w.wait()
@@ -108,16 +114,17 @@
         total = lax.fori_loop(0, picks_ref.shape[1], count, jnp.zeros((GRP, LANES), F32))
         counts_ref[step] = lane_sum(total)
     get_cols.wait()
-    for copy in get_rows:
+    for row, copy in enumerate(get_rows):
         copy.wait()
-    for slot in range(slots):
-        row = slots_ref[0, slot]
-        tiles = jnp.concatenate([wall[cols_ref[j, me * row_blocks + row]] for j in range(xv_ref.shape[1])], axis=1)
-        piece = lax.dot_general(
-            tiles, row_data(xv_ref, row), (((1,), (1,)), ((), ())), preferred_element_type=F32
-        )
-        for z, (low, high) in zip(zs, bounds, strict=True):
-            z[slot] = piece[low:high]
+
+        @pl.when(slot_of[row] >= 0)
+        def _(row=row):
+            tiles = jnp.concatenate([wall[cols_ref[j, me * row_blocks + row]] for j in range(xv_ref.shape[1])], axis=1)
+            piece = lax.dot_general(
+                tiles, row_data(xv_ref, row), (((1,), (1,)), ((), ())), preferred_element_type=F32
+            )
+            for z, (low, high) in zip(zs, bounds, strict=True):
+                z[slot_of[row]] = piece[low:high]
 
 
 def flip_kernel(x_ref, out_ref):
@@ -353,6 +360,7 @@
             pltpu.VMEM((col_blocks, classes, block_size), BF16),
             pltpu.SMEM(picks.shape, jnp.int32),
             pltpu.SMEM(cols.shape, jnp.int32),
+            pltpu.SMEM((row_blocks,), jnp.int32),
             pltpu.VMEM(gid_rows.shape, jnp.int32),
             pltpu.VMEM((classes, feat_rows), F32),
             pltpu.SemaphoreType.DMA((4 + row_blocks,)),

time: 248 us -> 249 us (level)
  no operation moved by 1% of the time
where the time goes in v3:
time: 249 us; the launch traced here: 248 us
  waiting for transfers between devices  154 us (62%)
  starting transfers between devices  67.5 us (27%)
  Pallas kernels  24.9 us (10%)
    ppermute x51, waiting for transfers between devices, swap(): return lax.ppermute(value, axis, [(i, i ^ mask) for i in range(count)])  154 us
    ppermute x51, starting transfers between devices, swap(): return lax.ppermute(value, axis, [(i, i ^ mask) for i in range(count)])  67.5 us
    pallas_call x6, Pallas kernels, evaluate(): pl.pallas_call(functools.partial(grad_kernel, step, n_samp, row_blocks, b...  9.92 us
    pallas_call x6, Pallas kernels, forward(): pl.pallas_call(functools.partial(forward_kernel, step, row_blocks), out_s...  8.44 us
  transfers between devices with their start and end apart: 51, of which 39 were waited for; matrix products, arithmetic and copies ran while one was open for 0% of the time, Pallas kernels for 0%

profile of v3, /device:TPU:0, one launch (start us, length us, event | category | flops | bytes accessed | tf_op | source)
XLA Modules:
  0.0 248.4 jit_solution(16147628283296765074)
XLA Ops:
  0.7 3.7 %setup.1 = (s32[3,5]{1,0:T(4,128)S(1)}, s32[3,5]{1,0:T(4,128)S(1)}, f32[3,8,128]{2,1,0:T(8,128)S(1)}, bf16[8,16,128,128]{3,2,1,0:T(8,128)(2,1)S(1)}, f32[8,64,12...) custom-call(s32[1]{0:T(128)} %bitcast.me_ref, s32[3,16]{1,0:T(4,128)} %picks_hbm.1, s32[16,32]{1,0:T(8,128)} %bitcast.6, ...), custom_call_target="tpu_custom_call" | custom-call | tf_op jit(solution)/shard_map/setup/pallas_call | solution.py:347
  8.8 4.5 %collective-permute-done.1.refs_1_ = f32[5,64,128]{2,1,0:T(8,128)S(1)} collective-permute-done((f32[5,64,128]{2,1,0:T(8,128)S(1)}, f32[5,64,128]{2,1,0:T(8,128)S(1)}, u32[]{:S(2)}, u32[]{:S(2)}) %collective-permute-start.1) | collective-permute-done | bytes 163872 | tf_op jit(solution)/shard_map/ppermute | solution.py:303
  15.0 4.5 %collective-permute-start.2 = (f32[520,128]{1,0:T(8,128)S(1)}, f32[520,128]{1,0:T(8,128)S(1)}, u32[]{:S(2)}, u32[]{:S(2)}) collective-permute-start(f32[520,128]{1,0:T(8,128)S(1)} %get-tuple-element.64), channel_id=1, source_target_pairs={{0,12},{4,8},{8,4},{12,0},{1,13},{5,9},{9,5},{13,1},{2,14},{6,10},... | collective-permute-start | bytes 798728 | tf_op jit(solution)/shard_map/ppermute | solution.py:303
  20.2 6.7 %collective-permute-done.2.refs_0_ = f32[520,128]{1,0:T(8,128)S(1)} collective-permute-done((f32[520,128]{1,0:T(8,128)S(1)}, f32[520,128]{1,0:T(8,128)S(1)}, u32[]{:S(2)}, u32[]{:S(2)}) %collective-permute-start.2) | collective-permute-done | bytes 266272 | tf_op jit(solution)/shard_map/ppermute | solution.py:303
  26.9 14.4 %collective-permute-done.3.refs_1_ = f32[520,128]{1,0:T(8,128)S(1)} collective-permute-done((f32[520,128]{1,0:T(8,128)S(1)}, f32[520,128]{1,0:T(8,128)S(1)}, u32[]{:S(2)}, u32[]{:S(2)}) %collective-permute-start.3) | collective-permute-done | bytes 266272 | tf_op jit(solution)/shard_map/ppermute | solution.py:303
  49.8 4.7 %collective-permute-done.6.refs_2_ = bf16[8,64,128]{2,1,0:T(8,128)(2,1)S(1)} collective-permute-done((bf16[8,64,128]{2,1,0:T(8,128)(2,1)S(1)}, bf16[8,64,128]{2,1,0:T(8,128)(2,1)S(1)}, u32[]{:S(2)}, u32[]{:S(2)}) %collective-permute-start.6) | collective-permute-done | bytes 131104 | tf_op jit(solution)/shard_map/ppermute | solution.py:303
  58.8 4.8 %collective-permute-done.9.refs_1_ = f32[5,64,128]{2,1,0:T(8,128)S(1)} collective-permute-done((f32[5,64,128]{2,1,0:T(8,128)S(1)}, f32[5,64,128]{2,1,0:T(8,128)S(1)}, u32[]{:S(2)}, u32[]{:S(2)}) %collective-permute-start.9) | collective-permute-done | bytes 163872 | tf_op jit(solution)/shard_map/ppermute | solution.py:303
  69.7 4.0 %collective-permute-done.10.refs_0_ = bf16[528,128]{1,0:T(8,128)(2,1)S(1)} collective-permute-done((bf16[528,128]{1,0:T(8,128)(2,1)S(1)}, bf16[528,128]{1,0:T(8,128)(2,1)S(1)}, u32[]{:S(2)}, u32[]{:S(2)}) %collective-permute-start.10) | collective-permute-done | bytes 135200 | tf_op jit(solution)/shard_map/ppermute | solution.py:303
  73.7 3.8 %collective-permute-done.11.refs_1_ = bf16[528,128]{1,0:T(8,128)(2,1)S(1)} collective-permute-done((bf16[528,128]{1,0:T(8,128)(2,1)S(1)}, bf16[528,128]{1,0:T(8,128)(2,1)S(1)}, u32[]{:S(2)}, u32[]{:S(2)}) %collective-permute-start.11) | collective-permute-done | bytes 135200 | tf_op jit(solution)/shard_map/ppermute | solution.py:303
  82.2 3.9 %collective-permute-done.15.refs_3_ = bf16[8,64,128]{2,1,0:T(8,128)(2,1)S(1)} collective-permute-done((bf16[8,64,128]{2,1,0:T(8,128)(2,1)S(1)}, bf16[8,64,128]{2,1,0:T(8,128)(2,1)S(1)}, u32[]{:S(2)}, u32[]{:S(2)}) %collective-permute-start.15) | collective-permute-done | bytes 131104 | tf_op jit(solution)/shard_map/ppermute | solution.py:303
  86.0 4.3 %collective-permute-done.14.refs_2_ = bf16[8,64,128]{2,1,0:T(8,128)(2,1)S(1)} collective-permute-done((bf16[8,64,128]{2,1,0:T(8,128)(2,1)S(1)}, bf16[8,64,128]{2,1,0:T(8,128)(2,1)S(1)}, u32[]{:S(2)}, u32[]{:S(2)}) %collective-permute-start.14) | collective-permute-done | bytes 131104 | tf_op jit(solution)/shard_map/ppermute | solution.py:303
  94.8 4.7 %collective-permute-done.17.refs_1_ = f32[5,64,128]{2,1,0:T(8,128)S(1)} collective-permute-done((f32[5,64,128]{2,1,0:T(8,128)S(1)}, f32[5,64,128]{2,1,0:T(8,128)S(1)}, u32[]{:S(2)}, u32[]{:S(2)}) %collective-permute-start.17) | collective-permute-done | bytes 163872 | tf_op jit(solution)/shard_map/ppermute | solution.py:303
  105.7 3.9 %collective-permute-done.18.refs_0_ = bf16[528,128]{1,0:T(8,128)(2,1)S(1)} collective-permute-done((bf16[528,128]{1,0:T(8,128)(2,1)S(1)}, bf16[528,128]{1,0:T(8,128)(2,1)S(1)}, u32[]{:S(2)}, u32[]{:S(2)}) %collective-permute-start.18) | collective-permute-done | bytes 135200 | tf_op jit(solution)/shard_map/ppermute | solution.py:303
  109.6 4.7 %collective-permute-done.19.refs_1_ = bf16[528,128]{1,0:T(8,128)(2,1)S(1)} collective-permute-done((bf16[528,128]{1,0:T(8,128)(2,1)S(1)}, bf16[528,128]{1,0:T(8,128)(2,1)S(1)}, u32[]{:S(2)}, u32[]{:S(2)}) %collective-permute-start.19) | collective-permute-done | bytes 135200 | tf_op jit(solution)/shard_map/ppermute | solution.py:303
  118.9 3.9 %collective-permute-done.23.refs_3_ = bf16[8,64,128]{2,1,0:T(8,128)(2,1)S(1)} collective-permute-done((bf16[8,64,128]{2,1,0:T(8,128)(2,1)S(1)}, bf16[8,64,128]{2,1,0:T(8,128)(2,1)S(1)}, u32[]{:S(2)}, u32[]{:S(2)}) %collective-permute-start.23) | collective-permute-done | bytes 131104 | tf_op jit(solution)/shard_map/ppermute | solution.py:303
  122.8 4.6 %collective-permute-done.22.refs_2_ = bf16[8,64,128]{2,1,0:T(8,128)(2,1)S(1)} collective-permute-done((bf16[8,64,128]{2,1,0:T(8,128)(2,1)S(1)}, bf16[8,64,128]{2,1,0:T(8,128)(2,1)S(1)}, u32[]{:S(2)}, u32[]{:S(2)}) %collective-permute-start.22) | collective-permute-done | bytes 131104 | tf_op jit(solution)/shard_map/ppermute | solution.py:303
  131.9 4.8 %collective-permute-done.25.refs_1_ = f32[5,64,128]{2,1,0:T(8,128)S(1)} collective-permute-done((f32[5,64,128]{2,1,0:T(8,128)S(1)}, f32[5,64,128]{2,1,0:T(8,128)S(1)}, u32[]{:S(2)}, u32[]{:S(2)}) %collective-permute-start.25) | collective-permute-done | bytes 163872 | tf_op jit(solution)/shard_map/ppermute | solution.py:303
  142.7 3.9 %collective-permute-done.26.refs_0_ = bf16[528,128]{1,0:T(8,128)(2,1)S(1)} collective-permute-done((bf16[528,128]{1,0:T(8,128)(2,1)S(1)}, bf16[528,128]{1,0:T(8,128)(2,1)S(1)}, u32[]{:S(2)}, u32[]{:S(2)}) %collective-permute-start.26) | collective-permute-done | bytes 135200 | tf_op jit(solution)/shard_map/ppermute | solution.py:303
  146.7 5.1 %collective-permute-done.27.refs_1_ = bf16[528,128]{1,0:T(8,128)(2,1)S(1)} collective-permute-done((bf16[528,128]{1,0:T(8,128)(2,1)S(1)}, bf16[528,128]{1,0:T(8,128)(2,1)S(1)}, u32[]{:S(2)}, u32[]{:S(2)}) %collective-permute-start.27) | collective-permute-done | bytes 135200 | tf_op jit(solution)/shard_map/ppermute | solution.py:303
  156.4 3.9 %collective-permute-done.31.refs_3_ = bf16[8,64,128]{2,1,0:T(8,128)(2,1)S(1)} collective-permute-done((bf16[8,64,128]{2,1,0:T(8,128)(2,1)S(1)}, bf16[8,64,128]{2,1,0:T(8,128)(2,1)S(1)}, u32[]{:S(2)}, u32[]{:S(2)}) %collective-permute-start.31) | collective-permute-done | bytes 131104 | tf_op jit(solution)/shard_map/ppermute | solution.py:303
  160.3 3.8 %collective-permute-done.30.refs_2_ = bf16[8,64,128]{2,1,0:T(8,128)(2,1)S(1)} collective-permute-done((bf16[8,64,128]{2,1,0:T(8,128)(2,1)S(1)}, bf16[8,64,128]{2,1,0:T(8,128)(2,1)S(1)}, u32[]{:S(2)}, u32[]{:S(2)}) %collective-permute-start.30) | collective-permute-done | bytes 131104 | tf_op jit(solution)/shard_map/ppermute | solution.py:303
  168.5 4.8 %collective-permute-done.33.refs_1_ = f32[5,64,128]{2,1,0:T(8,128)S(1)} collective-permute-done((f32[5,64,128]{2,1,0:T(8,128)S(1)}, f32[5,64,128]{2,1,0:T(8,128)S(1)}, u32[]{:S(2)}, u32[]{:S(2)}) %collective-permute-start.33) | collective-permute-done | bytes 163872 | tf_op jit(solution)/shard_map/ppermute | solution.py:303
  179.3 3.9 %collective-permute-done.34.refs_0_ = bf16[528,128]{1,0:T(8,128)(2,1)S(1)} collective-permute-done((bf16[528,128]{1,0:T(8,128)(2,1)S(1)}, bf16[528,128]{1,0:T(8,128)(2,1)S(1)}, u32[]{:S(2)}, u32[]{:S(2)}) %collective-permute-start.34) | collective-permute-done | bytes 135200 | tf_op jit(solution)/shard_map/ppermute | solution.py:303
  183.3 5.1 %collective-permute-done.35.refs_1_ = bf16[528,128]{1,0:T(8,128)(2,1)S(1)} collective-permute-done((bf16[528,128]{1,0:T(8,128)(2,1)S(1)}, bf16[528,128]{1,0:T(8,128)(2,1)S(1)}, u32[]{:S(2)}, u32[]{:S(2)}) %collective-permute-start.35) | collective-permute-done | bytes 135200 | tf_op jit(solution)/shard_map/ppermute | solution.py:303
  193.0 3.9 %collective-permute-done.39.refs_3_ = bf16[8,64,128]{2,1,0:T(8,128)(2,1)S(1)} collective-permute-done((bf16[8,64,128]{2,1,0:T(8,128)(2,1)S(1)}, bf16[8,64,128]{2,1,0:T(8,128)(2,1)S(1)}, u32[]{:S(2)}, u32[]{:S(2)}) %collective-permute-start.39) | collective-permute-done | bytes 131104 | tf_op jit(solution)/shard_map/ppermute | solution.py:303
  197.0 3.8 %collective-permute-done.38.refs_2_ = bf16[8,64,128]{2,1,0:T(8,128)(2,1)S(1)} collective-permute-done((bf16[8,64,128]{2,1,0:T(8,128)(2,1)S(1)}, bf16[8,64,128]{2,1,0:T(8,128)(2,1)S(1)}, u32[]{:S(2)}, u32[]{:S(2)}) %collective-permute-start.38) | collective-permute-done | bytes 131104 | tf_op jit(solution)/shard_map/ppermute | solution.py:303
  205.3 4.8 %collective-permute-done.41.refs_1_ = f32[5,64,128]{2,1,0:T(8,128)S(1)} collective-permute-done((f32[5,64,128]{2,1,0:T(8,128)S(1)}, f32[5,64,128]{2,1,0:T(8,128)S(1)}, u32[]{:S(2)}, u32[]{:S(2)}) %collective-permute-start.41) | collective-permute-done | bytes 163872 | tf_op jit(solution)/shard_map/ppermute | solution.py:303
  216.2 3.9 %collective-permute-done.42.refs_0_ = bf16[528,128]{1,0:T(8,128)(2,1)S(1)} collective-permute-done((bf16[528,128]{1,0:T(8,128)(2,1)S(1)}, bf16[528,128]{1,0:T(8,128)(2,1)S(1)}, u32[]{:S(2)}, u32[]{:S(2)}) %collective-permute-start.42) | collective-permute-done | bytes 135200 | tf_op jit(solution)/shard_map/ppermute | solution.py:303
  220.1 5.1 %collective-permute-done.43.refs_1_ = bf16[528,128]{1,0:T(8,128)(2,1)S(1)} collective-permute-done((bf16[528,128]{1,0:T(8,128)(2,1)S(1)}, bf16[528,128]{1,0:T(8,128)(2,1)S(1)}, u32[]{:S(2)}, u32[]{:S(2)}) %collective-permute-start.43) | collective-permute-done | bytes 135200 | tf_op jit(solution)/shard_map/ppermute | solution.py:303
  229.8 3.9 %collective-permute-done.47.refs_3_ = bf16[8,64,128]{2,1,0:T(8,128)(2,1)S(1)} collective-permute-done((bf16[8,64,128]{2,1,0:T(8,128)(2,1)S(1)}, bf16[8,64,128]{2,1,0:T(8,128)(2,1)S(1)}, u32[]{:S(2)}, u32[]{:S(2)}) %collective-permute-start.47) | collective-permute-done | bytes 131104 | tf_op jit(solution)/shard_map/ppermute | solution.py:303
  233.7 3.8 %collective-permute-done.46.refs_2_ = bf16[8,64,128]{2,1,0:T(8,128)(2,1)S(1)} collective-permute-done((bf16[8,64,128]{2,1,0:T(8,128)(2,1)S(1)}, bf16[8,64,128]{2,1,0:T(8,128)(2,1)S(1)}, u32[]{:S(2)}, u32[]{:S(2)}) %collective-permute-start.46) | collective-permute-done | bytes 131104 | tf_op jit(solution)/shard_map/ppermute | solution.py:303
  242.2 4.1 %collective-permute-done.49 = f32[8,32,128]{2,1,0:T(8,128)S(1)} collective-permute-done((f32[8,32,128]{2,1,0:T(8,128)S(1)}, f32[8,32,128]{2,1,0:T(8,128)S(1)}, u32[]{:S(2)}, u32[]{:S(2)}) %collective-permute-start.49) | collective-permute-done | bytes 131104 | tf_op jit(solution)/shard_map/ppermute | solution.py:303
  (107 shorter events, 97.7 us)
Async XLA Ops:
  15.0 11.9 %collective-permute-start.2 = (f32[520,128]{1,0:T(8,128)S(1)}, f32[520,128]{1,0:T(8,128)S(1)}, u32[]{:S(2)}, u32[]{:S(2)}) collective-permute-start(f32[520,128]{1,0:T(8,128)S(1)} %get-tuple-element.64), channel_id=1, source_target_pairs={{0,12},{4,8},{8,4},{12,0},{1,13},{5,9},{9,5},{13,1},{2,14},{6,10},... | collective-permute-start | bytes 798728 | tf_op jit(solution)/shard_map/ppermute | solution.py:303
  19.5 21.8 %collective-permute-start.3 = (f32[520,128]{1,0:T(8,128)S(1)}, f32[520,128]{1,0:T(8,128)S(1)}, u32[]{:S(2)}, u32[]{:S(2)}) collective-permute-start(f32[520,128]{1,0:T(8,128)S(1)} %get-tuple-element.65), channel_id=1, source_target_pairs={{0,8},{4,12},{8,0},{12,4},{1,9},{5,13},{9,1},{13,5},{2,10},{6,14},... | collective-permute-start | bytes 798728 | tf_op jit(solution)/shard_map/ppermute | solution.py:303
  19.5 21.8 %collective-permute-start.4 = (f32[520,128]{1,0:T(8,128)S(1)}, f32[520,128]{1,0:T(8,128)S(1)}, u32[]{:S(2)}, u32[]{:S(2)}) collective-permute-start(f32[520,128]{1,0:T(8,128)S(1)} %get-tuple-element.66), channel_id=1, source_target_pairs={{0,4},{4,0},{8,12},{12,8},{1,5},{5,1},{9,13},{13,9},{2,6},{6,2},{1... | collective-permute-start | bytes 798728 | tf_op jit(solution)/shard_map/ppermute | solution.py:303
  44.4 10.0 %collective-permute-start.6 = (bf16[8,64,128]{2,1,0:T(8,128)(2,1)S(1)}, bf16[8,64,128]{2,1,0:T(8,128)(2,1)S(1)}, u32[]{:S(2)}, u32[]{:S(2)}) collective-permute-start(bf16[8,64,128]{2,1,0:T(8,128)(2,1)S(1)} %get-tuple-element.68.refs_0_), channel_id=1, source_target_pairs={{0,8},{4,12},{8,0},{12,4},{1,9},{5,13},{9,1},{13,5},{2,10},{6,14},... | collective-permute-start | bytes 393224 | tf_op jit(solution)/shard_map/ppermute | solution.py:303
  44.4 10.0 %collective-permute-start.5 = (bf16[8,64,128]{2,1,0:T(8,128)(2,1)S(1)}, bf16[8,64,128]{2,1,0:T(8,128)(2,1)S(1)}, u32[]{:S(2)}, u32[]{:S(2)}) collective-permute-start(bf16[8,64,128]{2,1,0:T(8,128)(2,1)S(1)} %get-tuple-element.68.refs_0_), channel_id=1, source_target_pairs={{0,4},{4,0},{8,12},{12,8},{1,5},{5,1},{9,13},{13,9},{2,6},{6,2},{1... | collective-permute-start | bytes 393224 | tf_op jit(solution)/shard_map/ppermute | solution.py:303
  65.3 8.4 %collective-permute-start.10 = (bf16[528,128]{1,0:T(8,128)(2,1)S(1)}, bf16[528,128]{1,0:T(8,128)(2,1)S(1)}, u32[]{:S(2)}, u32[]{:S(2)}) collective-permute-start(bf16[528,128]{1,0:T(8,128)(2,1)S(1)} %get-tuple-element.71), channel_id=1, source_target_pairs={{0,12},{4,8},{8,4},{12,0},{1,13},{5,9},{9,5},{13,1},{2,14},{6,10},... | collective-permute-start | bytes 405512 | tf_op jit(solution)/shard_map/ppermute | solution.py:303
  66.3 11.2 %collective-permute-start.11 = (bf16[528,128]{1,0:T(8,128)(2,1)S(1)}, bf16[528,128]{1,0:T(8,128)(2,1)S(1)}, u32[]{:S(2)}, u32[]{:S(2)}) collective-permute-start(bf16[528,128]{1,0:T(8,128)(2,1)S(1)} %get-tuple-element.72), channel_id=1, source_target_pairs={{0,8},{4,12},{8,0},{12,4},{1,9},{5,13},{9,1},{13,5},{2,10},{6,14},... | collective-permute-start | bytes 405512 | tf_op jit(solution)/shard_map/ppermute | solution.py:303
  66.3 11.2 %collective-permute-start.12 = (bf16[528,128]{1,0:T(8,128)(2,1)S(1)}, bf16[528,128]{1,0:T(8,128)(2,1)S(1)}, u32[]{:S(2)}, u32[]{:S(2)}) collective-permute-start(bf16[528,128]{1,0:T(8,128)(2,1)S(1)} %get-tuple-element.73), channel_id=1, source_target_pairs={{0,4},{4,0},{8,12},{12,8},{1,5},{5,1},{9,13},{13,9},{2,6},{6,2},{1... | collective-permute-start | bytes 405512 | tf_op jit(solution)/shard_map/ppermute | solution.py:303
  79.7 10.7 %collective-permute-start.14 = (bf16[8,64,128]{2,1,0:T(8,128)(2,1)S(1)}, bf16[8,64,128]{2,1,0:T(8,128)(2,1)S(1)}, u32[]{:S(2)}, u32[]{:S(2)}) collective-permute-start(bf16[8,64,128]{2,1,0:T(8,128)(2,1)S(1)} %get-tuple-element.75.refs_0_), channel_id=1, source_target_pairs={{0,8},{4,12},{8,0},{12,4},{1,9},{5,13},{9,1},{13,5},{2,10},{6,14},... | collective-permute-start | bytes 393224 | tf_op jit(solution)/shard_map/ppermute | solution.py:303
  79.7 10.7 %collective-permute-start.13 = (bf16[8,64,128]{2,1,0:T(8,128)(2,1)S(1)}, bf16[8,64,128]{2,1,0:T(8,128)(2,1)S(1)}, u32[]{:S(2)}, u32[]{:S(2)}) collective-permute-start(bf16[8,64,128]{2,1,0:T(8,128)(2,1)S(1)} %get-tuple-element.75.refs_0_), channel_id=1, source_target_pairs={{0,4},{4,0},{8,12},{12,8},{1,5},{5,1},{9,13},{13,9},{2,6},{6,2},{1... | collective-permute-start | bytes 393224 | tf_op jit(solution)/shard_map/ppermute | solution.py:303
  103.7 10.6 %collective-permute-start.19 = (bf16[528,128]{1,0:T(8,128)(2,1)S(1)}, bf16[528,128]{1,0:T(8,128)(2,1)S(1)}, u32[]{:S(2)}, u32[]{:S(2)}) collective-permute-start(bf16[528,128]{1,0:T(8,128)(2,1)S(1)} %get-tuple-element.80), channel_id=1, source_target_pairs={{0,8},{4,12},{8,0},{12,4},{1,9},{5,13},{9,1},{13,5},{2,10},{6,14},... | collective-permute-start | bytes 405512 | tf_op jit(solution)/shard_map/ppermute | solution.py:303
  103.8 10.6 %collective-permute-start.20 = (bf16[528,128]{1,0:T(8,128)(2,1)S(1)}, bf16[528,128]{1,0:T(8,128)(2,1)S(1)}, u32[]{:S(2)}, u32[]{:S(2)}) collective-permute-start(bf16[528,128]{1,0:T(8,128)(2,1)S(1)} %get-tuple-element.81), channel_id=1, source_target_pairs={{0,4},{4,0},{8,12},{12,8},{1,5},{5,1},{9,13},{13,9},{2,6},{6,2},{1... | collective-permute-start | bytes 405512 | tf_op jit(solution)/shard_map/ppermute | solution.py:303
  116.7 10.7 %collective-permute-start.22 = (bf16[8,64,128]{2,1,0:T(8,128)(2,1)S(1)}, bf16[8,64,128]{2,1,0:T(8,128)(2,1)S(1)}, u32[]{:S(2)}, u32[]{:S(2)}) collective-permute-start(bf16[8,64,128]{2,1,0:T(8,128)(2,1)S(1)} %get-tuple-element.83.refs_0_), channel_id=1, source_target_pairs={{0,8},{4,12},{8,0},{12,4},{1,9},{5,13},{9,1},{13,5},{2,10},{6,14},... | collective-permute-start | bytes 393224 | tf_op jit(solution)/shard_map/ppermute | solution.py:303
  116.7 10.7 %collective-permute-start.21 = (bf16[8,64,128]{2,1,0:T(8,128)(2,1)S(1)}, bf16[8,64,128]{2,1,0:T(8,128)(2,1)S(1)}, u32[]{:S(2)}, u32[]{:S(2)}) collective-permute-start(bf16[8,64,128]{2,1,0:T(8,128)(2,1)S(1)} %get-tuple-element.83.refs_0_), channel_id=1, source_target_pairs={{0,4},{4,0},{8,12},{12,8},{1,5},{5,1},{9,13},{13,9},{2,6},{6,2},{1... | collective-permute-start | bytes 393224 | tf_op jit(solution)/shard_map/ppermute | solution.py:303
  138.3 8.4 %collective-permute-start.26 = (bf16[528,128]{1,0:T(8,128)(2,1)S(1)}, bf16[528,128]{1,0:T(8,128)(2,1)S(1)}, u32[]{:S(2)}, u32[]{:S(2)}) collective-permute-start(bf16[528,128]{1,0:T(8,128)(2,1)S(1)} %get-tuple-element.86), channel_id=1, source_target_pairs={{0,12},{4,8},{8,4},{12,0},{1,13},{5,9},{9,5},{13,1},{2,14},{6,10},... | collective-permute-start | bytes 405512 | tf_op jit(solution)/shard_map/ppermute | solution.py:303
  140.4 11.4 %collective-permute-start.27 = (bf16[528,128]{1,0:T(8,128)(2,1)S(1)}, bf16[528,128]{1,0:T(8,128)(2,1)S(1)}, u32[]{:S(2)}, u32[]{:S(2)}) collective-permute-start(bf16[528,128]{1,0:T(8,128)(2,1)S(1)} %get-tuple-element.87), channel_id=1, source_target_pairs={{0,8},{4,12},{8,0},{12,4},{1,9},{5,13},{9,1},{13,5},{2,10},{6,14},... | collective-permute-start | bytes 405512 | tf_op jit(solution)/shard_map/ppermute | solution.py:303
  140.4 11.4 %collective-permute-start.28 = (bf16[528,128]{1,0:T(8,128)(2,1)S(1)}, bf16[528,128]{1,0:T(8,128)(2,1)S(1)}, u32[]{:S(2)}, u32[]{:S(2)}) collective-permute-start(bf16[528,128]{1,0:T(8,128)(2,1)S(1)} %get-tuple-element.88), channel_id=1, source_target_pairs={{0,4},{4,0},{8,12},{12,8},{1,5},{5,1},{9,13},{13,9},{2,6},{6,2},{1... | collective-permute-start | bytes 405512 | tf_op jit(solution)/shard_map/ppermute | solution.py:303
  151.9 8.4 %collective-permute-start.31 = (bf16[8,64,128]{2,1,0:T(8,128)(2,1)S(1)}, bf16[8,64,128]{2,1,0:T(8,128)(2,1)S(1)}, u32[]{:S(2)}, u32[]{:S(2)}) collective-permute-start(bf16[8,64,128]{2,1,0:T(8,128)(2,1)S(1)} %get-tuple-element.90.refs_0_), channel_id=1, source_target_pairs={{0,12},{4,8},{8,4},{12,0},{1,13},{5,9},{9,5},{13,1},{2,14},{6,10},... | collective-permute-start | bytes 393224 | tf_op jit(solution)/shard_map/ppermute | solution.py:303
  153.4 10.7 %collective-permute-start.30 = (bf16[8,64,128]{2,1,0:T(8,128)(2,1)S(1)}, bf16[8,64,128]{2,1,0:T(8,128)(2,1)S(1)}, u32[]{:S(2)}, u32[]{:S(2)}) collective-permute-start(bf16[8,64,128]{2,1,0:T(8,128)(2,1)S(1)} %get-tuple-element.90.refs_0_), channel_id=1, source_target_pairs={{0,8},{4,12},{8,0},{12,4},{1,9},{5,13},{9,1},{13,5},{2,10},{6,14},... | collective-permute-start | bytes 393224 | tf_op jit(solution)/shard_map/ppermute | solution.py:303
  153.4 10.7 %collective-permute-start.29 = (bf16[8,64,128]{2,1,0:T(8,128)(2,1)S(1)}, bf16[8,64,128]{2,1,0:T(8,128)(2,1)S(1)}, u32[]{:S(2)}, u32[]{:S(2)}) collective-permute-start(bf16[8,64,128]{2,1,0:T(8,128)(2,1)S(1)} %get-tuple-element.90.refs_0_), channel_id=1, source_target_pairs={{0,4},{4,0},{8,12},{12,8},{1,5},{5,1},{9,13},{13,9},{2,6},{6,2},{1... | collective-permute-start | bytes 393224 | tf_op jit(solution)/shard_map/ppermute | solution.py:303
  174.9 8.4 %collective-permute-start.34 = (bf16[528,128]{1,0:T(8,128)(2,1)S(1)}, bf16[528,128]{1,0:T(8,128)(2,1)S(1)}, u32[]{:S(2)}, u32[]{:S(2)}) collective-permute-start(bf16[528,128]{1,0:T(8,128)(2,1)S(1)} %get-tuple-element.94), channel_id=1, source_target_pairs={{0,12},{4,8},{8,4},{12,0},{1,13},{5,9},{9,5},{13,1},{2,14},{6,10},... | collective-permute-start | bytes 405512 | tf_op jit(solution)/shard_map/ppermute | solution.py:303
  177.0 11.4 %collective-permute-start.35 = (bf16[528,128]{1,0:T(8,128)(2,1)S(1)}, bf16[528,128]{1,0:T(8,128)(2,1)S(1)}, u32[]{:S(2)}, u32[]{:S(2)}) collective-permute-start(bf16[528,128]{1,0:T(8,128)(2,1)S(1)} %get-tuple-element.95), channel_id=1, source_target_pairs={{0,8},{4,12},{8,0},{12,4},{1,9},{5,13},{9,1},{13,5},{2,10},{6,14},... | collective-permute-start | bytes 405512 | tf_op jit(solution)/shard_map/ppermute | solution.py:303
  177.0 11.4 %collective-permute-start.36 = (bf16[528,128]{1,0:T(8,128)(2,1)S(1)}, bf16[528,128]{1,0:T(8,128)(2,1)S(1)}, u32[]{:S(2)}, u32[]{:S(2)}) collective-permute-start(bf16[528,128]{1,0:T(8,128)(2,1)S(1)} %get-tuple-element.96), channel_id=1, source_target_pairs={{0,4},{4,0},{8,12},{12,8},{1,5},{5,1},{9,13},{13,9},{2,6},{6,2},{1... | collective-permute-start | bytes 405512 | tf_op jit(solution)/shard_map/ppermute | solution.py:303
  188.6 8.4 %collective-permute-start.39 = (bf16[8,64,128]{2,1,0:T(8,128)(2,1)S(1)}, bf16[8,64,128]{2,1,0:T(8,128)(2,1)S(1)}, u32[]{:S(2)}, u32[]{:S(2)}) collective-permute-start(bf16[8,64,128]{2,1,0:T(8,128)(2,1)S(1)} %get-tuple-element.98.refs_0_), channel_id=1, source_target_pairs={{0,12},{4,8},{8,4},{12,0},{1,13},{5,9},{9,5},{13,1},{2,14},{6,10},... | collective-permute-start | bytes 393224 | tf_op jit(solution)/shard_map/ppermute | solution.py:303
  190.4 10.3 %collective-permute-start.38 = (bf16[8,64,128]{2,1,0:T(8,128)(2,1)S(1)}, bf16[8,64,128]{2,1,0:T(8,128)(2,1)S(1)}, u32[]{:S(2)}, u32[]{:S(2)}) collective-permute-start(bf16[8,64,128]{2,1,0:T(8,128)(2,1)S(1)} %get-tuple-element.98.refs_0_), channel_id=1, source_target_pairs={{0,8},{4,12},{8,0},{12,4},{1,9},{5,13},{9,1},{13,5},{2,10},{6,14},... | collective-permute-start | bytes 393224 | tf_op jit(solution)/shard_map/ppermute | solution.py:303
  190.4 10.3 %collective-permute-start.37 = (bf16[8,64,128]{2,1,0:T(8,128)(2,1)S(1)}, bf16[8,64,128]{2,1,0:T(8,128)(2,1)S(1)}, u32[]{:S(2)}, u32[]{:S(2)}) collective-permute-start(bf16[8,64,128]{2,1,0:T(8,128)(2,1)S(1)} %get-tuple-element.98.refs_0_), channel_id=1, source_target_pairs={{0,4},{4,0},{8,12},{12,8},{1,5},{5,1},{9,13},{13,9},{2,6},{6,2},{1... | collective-permute-start | bytes 393224 | tf_op jit(solution)/shard_map/ppermute | solution.py:303
  211.7 8.4 %collective-permute-start.42 = (bf16[528,128]{1,0:T(8,128)(2,1)S(1)}, bf16[528,128]{1,0:T(8,128)(2,1)S(1)}, u32[]{:S(2)}, u32[]{:S(2)}) collective-permute-start(bf16[528,128]{1,0:T(8,128)(2,1)S(1)} %get-tuple-element.101), channel_id=1, source_target_pairs={{0,12},{4,8},{8,4},{12,0},{1,13},{5,9},{9,5},{13,1},{2,14},{6,10},... | collective-permute-start | bytes 405512 | tf_op jit(solution)/shard_map/ppermute | solution.py:303
  213.8 11.4 %collective-permute-start.43 = (bf16[528,128]{1,0:T(8,128)(2,1)S(1)}, bf16[528,128]{1,0:T(8,128)(2,1)S(1)}, u32[]{:S(2)}, u32[]{:S(2)}) collective-permute-start(bf16[528,128]{1,0:T(8,128)(2,1)S(1)} %get-tuple-element.102), channel_id=1, source_target_pairs={{0,8},{4,12},{8,0},{12,4},{1,9},{5,13},{9,1},{13,5},{2,10},{6,14},... | collective-permute-start | bytes 405512 | tf_op jit(solution)/shard_map/ppermute | solution.py:303
  213.8 11.4 %collective-permute-start.44 = (bf16[528,128]{1,0:T(8,128)(2,1)S(1)}, bf16[528,128]{1,0:T(8,128)(2,1)S(1)}, u32[]{:S(2)}, u32[]{:S(2)}) collective-permute-start(bf16[528,128]{1,0:T(8,128)(2,1)S(1)} %get-tuple-element.103), channel_id=1, source_target_pairs={{0,4},{4,0},{8,12},{12,8},{1,5},{5,1},{9,13},{13,9},{2,6},{6,2},{1... | collective-permute-start | bytes 405512 | tf_op jit(solution)/shard_map/ppermute | solution.py:303
  225.3 8.4 %collective-permute-start.47 = (bf16[8,64,128]{2,1,0:T(8,128)(2,1)S(1)}, bf16[8,64,128]{2,1,0:T(8,128)(2,1)S(1)}, u32[]{:S(2)}, u32[]{:S(2)}) collective-permute-start(bf16[8,64,128]{2,1,0:T(8,128)(2,1)S(1)} %get-tuple-element.104.refs_0_), channel_id=1, source_target_pairs={{0,12},{4,8},{8,4},{12,0},{1,13},{5,9},{9,5},{13,1},{2,14},{6,10},... | collective-permute-start | bytes 393224 | tf_op jit(solution)/shard_map/ppermute | solution.py:303
  227.2 10.3 %collective-permute-start.46 = (bf16[8,64,128]{2,1,0:T(8,128)(2,1)S(1)}, bf16[8,64,128]{2,1,0:T(8,128)(2,1)S(1)}, u32[]{:S(2)}, u32[]{:S(2)}) collective-permute-start(bf16[8,64,128]{2,1,0:T(8,128)(2,1)S(1)} %get-tuple-element.104.refs_0_), channel_id=1, source_target_pairs={{0,8},{4,12},{8,0},{12,4},{1,9},{5,13},{9,1},{13,5},{2,10},{6,14},... | collective-permute-start | bytes 393224 | tf_op jit(solution)/shard_map/ppermute | solution.py:303
  227.2 10.3 %collective-permute-start.45 = (bf16[8,64,128]{2,1,0:T(8,128)(2,1)S(1)}, bf16[8,64,128]{2,1,0:T(8,128)(2,1)S(1)}, u32[]{:S(2)}, u32[]{:S(2)}) collective-permute-start(bf16[8,64,128]{2,1,0:T(8,128)(2,1)S(1)} %get-tuple-element.104.refs_0_), channel_id=1, source_target_pairs={{0,4},{4,0},{8,12},{12,8},{1,5},{5,1},{9,13},{13,9},{2,6},{6,2},{1... | collective-permute-start | bytes 393224 | tf_op jit(solution)/shard_map/ppermute | solution.py:303
  (22 other events, 127.8 us)
